TPU v7x, 128 devices: a whole 4x4x4 slice. The times are simulated.
128 devices in a mesh: cfg: 2 (over y_hi), group: 16 (over y_lo, x, core), mp: 4 (over z).
Axes of the slice: x: 4, y: 4 (y_hi: 2, y_lo: 2; y = y_hi * 2 + y_lo), z: 4, core: 2. Of those that a mesh axis runs over, the one named last changes fastest.
Arguments:
- latents: float32 [16384, 64], P(('group', 'mp')), may hold values from -0.6 to 0.6
- text_hidden: bfloat16 [2, 8192, 3072], P('cfg', ('group', 'mp')), may hold values from -6 to 6
- w_img_in: bfloat16 [64, 3072], replicated, may hold values from -0.75 to 0.75
- w_img_qkv: bfloat16 [3072, 4608], P(None, 'mp'), may hold values from -1 to 1
- w_txt_kv: bfloat16 [3072, 3072], P(None, 'mp'), may hold values from -0.109375 to 0.109375
- q_gain: float32 [128], replicated, may hold values from 0.25 to 1.75
- k_gain: float32 [128], replicated, may hold values from 0.25 to 1.75
- w_out: bfloat16 [1536, 3072], replicated, may hold values from -1 to 1
- w_final: bfloat16 [3072, 64], replicated, may hold values from -0.109375 to 0.109375
- mod_img: float32 [8, 3, 3072], replicated, may hold values from -3 to 3
- mod_txt: float32 [8, 2, 3072], replicated, may hold values from -3 to 3
- mod_final: float32 [8, 2, 3072], replicated, may hold values from -3 to 3
- guide: float32 [16], replicated, may hold values from 1.5 to 5
- step_size: float32 [8], replicated, may hold values from 0.02 to 0.3
- img_len: int32 [16], replicated, may hold values from 1 to 1024, as said below
- txt_len: int32 [16], replicated, may hold values from 1 to 512, as said below
- split_flag: int32 [2, 16], replicated, may hold values from 0 to 1, as said below
- tstep: int32 [16], replicated, may hold values from 0 to 7
Outputs:
- velocity: float32 [2, 8192, 64], P('cfg', ('group', 'mp'))
- next_latents: float32 [2, 8192, 64], P('cfg', ('group', 'mp'))
Inputs may be any that keep to these rules, and one draw needn't show every extreme that they name: `img_len`: some group has exactly 1024 live image tokens. `txt_len`: some group has exactly 512 live text tokens. `split_flag`: entries [c, 2j] and [c, 2j + 1] are equal; at least one such pair carries 1 and at least one carries 0.
All inputs are finite; a program needn't handle non-finite values.
Results may differ from a plain program's by a relative error of at most 0.035.
Values may be sent and summed in bfloat16 or wider, within the bound.
A program may use at most 192 MiB of HBM per device.

v0:
```python
import jax
import jax.numpy as jnp
from jax import lax
from jax.sharding import PartitionSpec as P

HD = 128


def partner(value, axis, bit):
    mask = 2**bit
    pairs = [(source, source ^ mask) for source in range(lax.axis_size(axis))]
    return lax.ppermute(value, axis, pairs)


def layer_norm(values):
    center = values - jnp.mean(values, -1, keepdims=True)
    spread = jnp.mean(center * center, -1, keepdims=True)
    return center * lax.rsqrt(spread + 1e-06)


def head_norm(values, gain):
    return values * lax.rsqrt(jnp.mean(values * values, -1, keepdims=True) + 1e-06) * gain


def pick_entry(table, index):
    return lax.dynamic_index_in_dim(table, index, 0, keepdims=False)


def local(
    latents,
    text_hidden,
    w_img_in,
    w_img_qkv,
    w_txt_kv,
    q_gain,
    k_gain,
    w_out,
    w_final,
    mod_img,
    mod_txt,
    mod_final,
    guide,
    step_size,
    img_len,
    txt_len,
    split_flag,
    tstep,
):
    group_index = lax.axis_index("group")
    mp_index = lax.axis_index("mp")
    cfg_index = lax.axis_index("cfg")
    mp_count = lax.axis_size("mp")
    mate_index = jnp.bitwise_xor(group_index, 1)
    step_index = pick_entry(tstep, group_index)
    mod_rows = pick_entry(mod_img, step_index)
    text_rows = pick_entry(mod_txt, step_index)
    final_rows = pick_entry(mod_final, step_index)
    shard_rows = latents.shape[0]
    half_rows = shard_rows // 2
    full_img = shard_rows * mp_count
    full_txt = text_hidden.shape[1] * mp_count
    local_heads = w_img_qkv.shape[1] // (3 * HD)
    x_img = jnp.dot(latents.astype(jnp.bfloat16), w_img_in, preferred_element_type=jnp.float32)
    img_mod = (layer_norm(x_img) * (1.0 + mod_rows[1]) + mod_rows[0]).astype(jnp.bfloat16)
    txt_mod = (
        layer_norm(text_hidden[0].astype(jnp.float32)) * (1.0 + text_rows[1]) + text_rows[0]
    ).astype(jnp.bfloat16)
    img_full, txt_full = (
        lax.all_gather(img_mod, "mp", axis=0, tiled=True),
        lax.all_gather(txt_mod, "mp", axis=0, tiled=True),
    )
    qkv = jnp.dot(img_full, w_img_qkv, preferred_element_type=jnp.float32).reshape(
        full_img, local_heads, 3, HD
    )
    query = head_norm(qkv[:, :, 0], q_gain).astype(jnp.bfloat16)
    key_img = head_norm(qkv[:, :, 1], k_gain).astype(jnp.bfloat16)
    value_img = qkv[:, :, 2].astype(jnp.bfloat16)
    text_kv = jnp.dot(txt_full, w_txt_kv, preferred_element_type=jnp.float32).reshape(
        full_txt, local_heads, 2, HD
    )
    key_txt = head_norm(text_kv[:, :, 0], k_gain).astype(jnp.bfloat16)
    value_txt = text_kv[:, :, 1].astype(jnp.bfloat16)
    key_rows = jnp.concatenate([key_txt, key_img], axis=0)
    value_rows = jnp.concatenate([value_txt, value_img], axis=0)
    mate_keys, mate_values = partner((key_rows, value_rows), "group", 0)
    spots_txt = jnp.arange(full_txt, dtype=jnp.int32)
    spots_img = jnp.arange(full_img, dtype=jnp.int32)

    def live_rows(index):
        return jnp.concatenate(
            [spots_txt < pick_entry(txt_len, index), spots_img < pick_entry(img_len, index)]
        )

    flagged = pick_entry(pick_entry(split_flag, cfg_index), group_index) == 1
    live = jnp.concatenate([live_rows(group_index), live_rows(mate_index) & flagged])
    all_keys = jnp.concatenate([key_rows, mate_keys], axis=0)
    all_values = jnp.concatenate([value_rows, mate_values], axis=0)
    scores = jnp.einsum(
        "qhe,khe->hqk", query, all_keys, preferred_element_type=jnp.float32
    ) * HD ** (-0.5)
    scores = jnp.where(live[None, None, :], scores, -1e30)
    weights = jnp.exp(scores - jnp.max(scores, -1, keepdims=True))
    probs = (weights / jnp.sum(weights, -1, keepdims=True)).astype(jnp.bfloat16)
    mixed = jnp.einsum(
        "hqk,khe->qhe", probs, all_values, preferred_element_type=jnp.float32
    ).astype(jnp.bfloat16)
    mixed = mixed.reshape(full_img, local_heads * HD)
    w_local = lax.dynamic_slice_in_dim(w_out, mp_index * local_heads * HD, local_heads * HD, 0)
    attended = lax.psum_scatter(
        jnp.dot(mixed, w_local, preferred_element_type=jnp.float32),
        "mp",
        scatter_dimension=0,
        tiled=True,
    )
    hidden = x_img + mod_rows[2] * attended
    final = (layer_norm(hidden) * (1.0 + final_rows[1]) + final_rows[0]).astype(jnp.bfloat16)
    own_velocity = jnp.dot(final, w_final, preferred_element_type=jnp.float32)
    scale = pick_entry(guide, group_index)
    other_velocity = partner(own_velocity.astype(jnp.bfloat16), "cfg", 0).astype(own_velocity.dtype)
    is_cond = cfg_index == 0
    cond_part = jnp.where(is_cond, own_velocity, other_velocity)
    uncond_part = jnp.where(is_cond, other_velocity, own_velocity)
    guided_all = uncond_part + scale * (cond_part - uncond_part)
    guided = lax.dynamic_slice_in_dim(guided_all, cfg_index * half_rows, half_rows, 0)
    row_place = (
        mp_index * shard_rows + cfg_index * half_rows + jnp.arange(half_rows, dtype=jnp.int32)
    )
    row_live = row_place < pick_entry(img_len, group_index)
    guided = jnp.where(row_live[:, None], guided, 0.0)
    start_rows = lax.dynamic_slice_in_dim(latents, cfg_index * half_rows, half_rows, 0)
    moved = start_rows - pick_entry(step_size, step_index) * guided
    return (guided[None], moved[None])


def solution(mesh):
    placed = (
        P(("group", "mp"), None),
        P("cfg", ("group", "mp"), None),
        P(),
        P(None, "mp"),
        P(None, "mp"),
        P(),
        P(),
        P(),
        P(),
        P(),
        P(),
        P(),
        P(),
        P(),
        P(),
        P(),
        P(),
        P(),
    )
    return jax.shard_map(
        local,
        mesh=mesh,
        in_specs=placed,
        out_specs=(P("cfg", ("group", "mp"), None), P("cfg", ("group", "mp"), None)),
        check_vma=False,
    )
```

profile of v0, /device:TPU:0, one launch (start us, length us, event | category | flops | bytes accessed | tf_op | source)
XLA Modules:
  0.0 342.3 jit_solution(17559711383967402021)
XLA Ops:
  14.3 2.4 fusion.21
  18.8 1.6 constant_dynamic-slice_fusion
  20.3 1.8 add_convert_fusion.1
  25.1 34.0 %all-gather.3.cloned.1.call-done = bf16[512,3072]{1,0:T(8,128)(2,1)} async-done(((bf16[128,3072]{1,0:T(8,128)(2,1)}), bf16[512,3072]{1,0:T(8,128)(2,1)}) %all-gather.3.cloned.1.call-update) | async-done | bytes 3145744 | tf_op jit(solution)/shard_map/all_gather | solution.py:70
  59.1 7.0 %fusion.53 = f32[512,768]{1,0:T(8,128)} fusion(bf16[512,3072]{1,0:T(8,128)(2,1)} %all-gather.3.cloned.1.call-done, bf16[3072,768]{1,0:T(8,128)(2,1)} %param.22), kind=kOutput, calls=%fused_computation.97 | convolution fusion | flops 2415919104 | bytes 9437184 | tf_op jit(solution)/shard_map/dot_general | solution.py:78
  66.1 2.9 reshape.125
  69.1 2.1 slice.60
  71.8 55.0 %all-gather.5.cloned.1.call-done = bf16[1024,3072]{1,0:T(8,128)(2,1)} async-done(((bf16[256,3072]{1,0:T(8,128)(2,1)}), bf16[1024,3072]{1,0:T(8,128)(2,1)}) %all-gather.5.cloned.1.call-update) | async-done | bytes 6291472 | tf_op jit(solution)/shard_map/all_gather | solution.py:69
  126.8 11.3 %fusion.54 = f32[1024,1152]{0,1:T(8,128)S(1)} fusion(bf16[1024,3072]{1,0:T(8,128)(2,1)} %all-gather.5.cloned.1.call-done, bf16[3072,1152]{1,0:T(8,128)(2,1)} %param.21), kind=kOutput, calls=%fused_computation.98 | convolution fusion | flops 7247757312 | bytes 18087936 | tf_op jit(solution)/shard_map/dot_general | solution.py:72
  138.1 2.1 copy-done.2
  141.5 3.0 copy.40
  144.5 1.9 fusion.22
  146.4 1.9 fusion.24
  153.5 3.1 slice.57
  156.6 2.9 copy.41
  161.9 2.1 pad_maximum_fusion.1
  164.5 1.6 multiply_reduce_fusion.2
  166.1 19.6 %fusion.51 = (f32[3,1024]{1,0:T(4,128)}, f32[3,1024,3072]{2,1,0:T(8,128)}) fusion(pred[3072]{0:T(1024)(128)(4,1)} %pad_add_fusion, bf16[1536,3,128]{2,0,1:T(8,128)(2,1)} %collective-permute-done.1, bf16[1024,3,128]{2,0,1:T(8,128)(2,1)} %copy-done.4, bf16[512,3,128]{2,0,1:T(8,128)(2,1)S(1)} %multiply_convert_fusion.1, f32[1024,3,3,128]{0,3,2,1:T(8,128)} %bitcast.91, ...), kind=kOutput, calls=%fused_computation.95 | convolution fusion | flops 2461928448 | bytes 41709056 | tf_op jit(solution)/shard_map/sub | solution.py:102
  185.7 15.0 %fusion.26 = bf16[3,128,1024]{2,1,0:T(8,128)(2,1)S(1)} fusion(f32[3,1024,3072]{2,1,0:T(8,128)} %get-tuple-element.19, f32[3,1024]{1,0:T(4,128)} %get-tuple-element.18, bf16[1536,3,128]{0,2,1:T(8,128)(2,1)} %collective-permute-done, bf16[1024,3,128]{0,2,1:T(8,128)(2,1)} %copy-done.3, bf16[512,3,128]{0,2,1:T(8,128)(2,1)} %bitcast.93), kind=kOutput, calls=%fused_computation.42 | convolution fusion | flops 2442264576 | bytes 40906752 | tf_op jit(solution)/shard_map/hqk,khe->qhe/dot_general | solution.py:104
  200.7 8.1 %fusion.13 = f32[1024,3072]{1,0:T(8,128)} fusion(bf16[1024,384]{0,1:T(8,128)(2,1)S(1)} %bitcast.94, bf16[1536,3072]{1,0:T(8,128)(2,1)} %param.25, s32[]{:T(128)S(6)} %select_n.66), kind=kOutput, calls=%fused_computation.21 | convolution fusion | flops 2415919104 | bytes 15728644 | tf_op jit(solution)/shard_map/dot_general | solution.py:110
  210.3 113.9 %reduce-scatter.2.cloned.1.call-done = f32[256,3072]{1,0:T(8,128)} async-done(((f32[1024,3072]{1,0:T(8,128)}), f32[256,3072]{1,0:T(8,128)}) %reduce-scatter.2.cloned.1.call-update) | async-done | bytes 3145744 | tf_op jit(solution)/shard_map/reduce_scatter | solution.py:109
  324.2 2.3 fusion.47
  328.4 3.1 collective-permute-start.2
  333.9 1.9 subtract_bitcast_fusion
  (72 shorter events, 25.0 us)
Async XLA Ops:
  7.2 9.6 %copy-start = (bf16[64,3072]{1,0:T(8,128)(2,1)S(1)}, bf16[64,3072]{1,0:T(8,128)(2,1)}, u32[]{:S(2)}) copy-start(bf16[64,3072]{1,0:T(8,128)(2,1)} %param.20) | copy-start | bytes 1179652
  7.2 51.9 %all-gather.3.cloned.1.call-start = ((), (), s32[]{:S(2)}) async-start(), calls=%async_computation.1 | async-start | bytes 3932160 | tf_op jit(solution)/shard_map/all_gather | solution.py:70
  16.7 110.0 %all-gather.5.cloned.1.call-start = ((), (), s32[]{:S(2)}) async-start(), calls=%async_computation.2 | async-start | bytes 7864320 | tf_op jit(solution)/shard_map/all_gather | solution.py:69
  20.3 2.1 copy-start.8
  20.3 2.1 copy-start.9
  22.2 302.0 %reduce-scatter.2.cloned.1.call-start = ((), (), s32[]{:S(2)}) async-start(), calls=%async_computation.3 | async-start | bytes 15728640 | tf_op jit(solution)/shard_map/reduce_scatter | solution.py:109
  66.1 5.3 %copy-start.10 = (f32[128]{0:T(128)S(1)}, f32[128]{0:T(128)}, u32[]{:S(2)}) copy-start(f32[128]{0:T(128)} %param.24) | copy-start | bytes 1540
  138.1 2.2 copy-start.2
  148.3 0.9 copy-start.4
  150.3 15.8 %collective-permute-start.1 = (bf16[1536,3,128]{2,0,1:T(8,128)(2,1)}, bf16[1536,3,128]{2,0,1:T(8,128)(2,1)}, u32[]{:S(2)}, u32[]{:S(2)}) collective-permute-start(bf16[1536,3,128]{2,0,1:T(8,128)(2,1)} %pad_maximum_fusion.2), channel_id=1, source_target_pairs={{0,4},{4,0},{8,12},{12,8},{16,20},{20,16},{24,28},{28,24},{32,36},... | collective-permute-start | bytes 3538952 | tf_op jit(solution)/shard_map/ppermute | solution.py:12
  161.0 0.9 copy-start.3
  164.0 21.7 %collective-permute-start = (bf16[1536,3,128]{0,2,1:T(8,128)(2,1)}, bf16[1536,3,128]{0,2,1:T(8,128)(2,1)}, u32[]{:S(2)}, u32[]{:S(2)}) collective-permute-start(bf16[1536,3,128]{0,2,1:T(8,128)(2,1)} %pad_maximum_fusion.1), channel_id=1, source_target_pairs={{0,4},{4,0},{8,12},{12,8},{16,20},{20,16},{24,28},{28,24},{32,36},... | collective-permute-start | bytes 3538952 | tf_op jit(solution)/shard_map/ppermute | solution.py:12
  208.8 115.4 %copy-start.6 = (f32[1,1,3072]{2,0,1:T(1,128)S(1)}, f32[1,1,3072]{2,0,1:T(1,128)}, u32[]{:S(2)}) copy-start(f32[1,1,3072]{2,0,1:T(1,128)} %get-tuple-element.4) | copy-start | bytes 36868
  326.6 0.7 copy-start.7
  326.6 1.1 copy-start.11
  326.6 9.2 %copy-start.1 = (bf16[64,3072]{1,0:T(8,128)(2,1)S(1)}, bf16[64,3072]{1,0:T(8,128)(2,1)}, u32[]{:S(2)}) copy-start(bf16[64,3072]{1,0:T(8,128)(2,1)} %param.20) | copy-start | bytes 1179652
  326.6 5.6 %copy-start.12 = (f32[8]{0:T(128)S(1)}, f32[8]{0:T(128)}, u32[]{:S(2)}) copy-start(f32[8]{0:T(128)} %param.31) | copy-start | bytes 100
  326.6 6.3 %copy-start.13 = (f32[16]{0:T(128)S(1)}, f32[16]{0:T(128)}, u32[]{:S(2)}) copy-start(f32[16]{0:T(128)} %param.30) | copy-start | bytes 196
  326.6 7.3 %copy-start.5 = (f32[256,64]{0,1:T(8,128)S(1)}, f32[256,64]{0,1:T(8,128)}, u32[]{:S(2)}) copy-start(f32[256,64]{0,1:T(8,128)} %param.18) | copy-start | bytes 196612
  328.4 5.5 %collective-permute-start.2 = (bf16[256,64]{0,1:T(8,128)(2,1)S(1)}, bf16[256,64]{0,1:T(8,128)(2,1)S(1)}, u32[]{:S(2)}, u32[]{:S(2)}) collective-permute-start(bf16[256,64]{0,1:T(8,128)(2,1)S(1)} %get-tuple-element.20), channel_id=1, source_target_pairs={{0,64},{64,0},{1,65},{65,1},{2,66},{66,2},{3,67},{67,3},{4,68},{68... | collective-permute-start | bytes 98312 | tf_op jit(solution)/shard_map/ppermute | solution.py:12
Sparse Core Ops, SparseCore 0:
  16.8 42.2 all-gather.2
  60.8 65.9 all-gather.4
  209.0 115.2 reduce-scatter.1
where the time goes:
time: 343 us; the launch traced here: 342 us
  waiting for transfers between devices  203 us (59%)
  matrix products  63.3 us (18%)
  other arithmetic  27.7 us (8%)
  local copies, waits for them, and re-layouts  27.4 us (8%)
  between operations  16.7 us (5%)
  starting transfers between devices  3.9 us (1%)
    reduce_scatter x1, waiting for transfers between devices, local(): lax.psum_scatter(jnp.dot(mixed, w_local, preferred_element_type=jnp.float...  114 us
    all_gather x1, waiting for transfers between devices, local(): lax.all_gather(img_mod, 'mp', axis=0, tiled=True)  55 us
    all_gather x1, waiting for transfers between devices, local(): lax.all_gather(txt_mod, 'mp', axis=0, tiled=True)  34 us
    sub x1, matrix products, local(): weights = jnp.exp(scores - jnp.max(scores, -1, keepdims=True))  19.6 us
    dot_general x1, matrix products, local(): jnp.einsum('hqk,khe->qhe', probs, all_values, preferred_element_type=jnp....  15 us
    dot_general x1, matrix products, local(): jnp.dot(img_full, w_img_qkv, preferred_element_type=jnp.float32)  11.3 us
    unnamed x30, local copies, waits for them, and re-layouts  10.4 us
    dot_general x1, matrix products, local(): jnp.dot(mixed, w_local, preferred_element_type=jnp.float32)  8.09 us
  transfers between devices with their start and end apart: 6, of which 4 were waited for; matrix products, arithmetic and copies ran while one was open for 17% of the time, Pallas kernels for 0%

commit v1 on v0

--- a/solution.py
+++ b/solution.py
@@ -61,14 +61,13 @@
     full_txt = text_hidden.shape[1] * mp_count
     local_heads = w_img_qkv.shape[1] // (3 * HD)
     x_img = jnp.dot(latents.astype(jnp.bfloat16), w_img_in, preferred_element_type=jnp.float32)
-    img_mod = (layer_norm(x_img) * (1.0 + mod_rows[1]) + mod_rows[0]).astype(jnp.bfloat16)
+    lat_full = lax.all_gather(latents.astype(jnp.bfloat16), "mp", axis=0, tiled=True)
+    x_full = jnp.dot(lat_full, w_img_in, preferred_element_type=jnp.float32)
+    img_full = (layer_norm(x_full) * (1.0 + mod_rows[1]) + mod_rows[0]).astype(jnp.bfloat16)
     txt_mod = (
         layer_norm(text_hidden[0].astype(jnp.float32)) * (1.0 + text_rows[1]) + text_rows[0]
     ).astype(jnp.bfloat16)
-    img_full, txt_full = (
-        lax.all_gather(img_mod, "mp", axis=0, tiled=True),
-        lax.all_gather(txt_mod, "mp", axis=0, tiled=True),
-    )
+    txt_full = lax.all_gather(txt_mod, "mp", axis=0, tiled=True)
     qkv = jnp.dot(img_full, w_img_qkv, preferred_element_type=jnp.float32).reshape(
         full_img, local_heads, 3, HD
     )
@@ -105,13 +104,8 @@
         "hqk,khe->qhe", probs, all_values, preferred_element_type=jnp.float32
     ).astype(jnp.bfloat16)
     mixed = mixed.reshape(full_img, local_heads * HD)
-    w_local = lax.dynamic_slice_in_dim(w_out, mp_index * local_heads * HD, local_heads * HD, 0)
-    attended = lax.psum_scatter(
-        jnp.dot(mixed, w_local, preferred_element_type=jnp.float32),
-        "mp",
-        scatter_dimension=0,
-        tiled=True,
-    )
+    mixed = lax.all_to_all(mixed, "mp", split_axis=0, concat_axis=1, tiled=True)
+    attended = jnp.dot(mixed, w_out, preferred_element_type=jnp.float32)
     hidden = x_img + mod_rows[2] * attended
     final = (layer_norm(hidden) * (1.0 + final_rows[1]) + final_rows[0]).astype(jnp.bfloat16)
     own_velocity = jnp.dot(final, w_final, preferred_element_type=jnp.float32)

time: 343 us -> 163 us (0.48)
  waiting for transfers between devices: 203 us -> 12.8 us
  blocking collectives: 0 us -> 13.3 us
  local copies, waits for them, and re-layouts: 27.4 us -> 17 us
  matrix products: 63.3 us -> 68.8 us
  starting transfers between devices: 3.9 us -> 8.17 us
    reduce_scatter x1 -> x0, waiting for transfers between devices: 114 us -> none  [local(): lax.psum_scatter(jnp.dot(mixed, w_local, preferred_element_type=jnp.float...]
    all_gather x2 -> x1, waiting for transfers between devices: 89 us -> 0.02 us  [local(): txt_full = lax.all_gather(txt_mod, 'mp', axis=0, tiled=True)]
    all_gather x0 -> x1, blocking collectives: none -> 13.3 us  [local(): lax.all_gather(latents.astype(jnp.bfloat16), 'mp', axis=0, tiled=True)]
    all_to_all x0 -> x1, waiting for transfers between devices: none -> 12.5 us  [local(): mixed = lax.all_to_all(mixed, 'mp', split_axis=0, concat_axis=1, tiled=True)]
    unnamed x30 -> x34, local copies, waits for them, and re-layouts: 10.4 us -> 4.78 us
    reduce_sum x3, other arithmetic: 2.41 us -> 7.98 us  [layer_norm(): spread = jnp.mean(center * center, -1, keepdims=True)]
    all_to_all x0 -> x1, starting transfers between devices: none -> 4.26 us  [local(): mixed = lax.all_to_all(mixed, 'mp', split_axis=0, concat_axis=1, tiled=True)]
    dot_general x1 -> x2, matrix products: 8.09 us -> 11.6 us  [the longest x1 6.4 us: local(): x_full = jnp.dot(lat_full, w_img_in, preferred_element_type=jnp.float32)]
  transfers between devices with their start and end apart: 6 -> 5, of which waited for: 4 -> 2; matrix products, arithmetic and copies ran while one was open for 17% -> 38% of each run, Pallas kernels for 0% -> 0%
where the time goes in v1:
time: 163 us; the launch traced here: 162 us
  matrix products  68.8 us (42%)
  other arithmetic  24.9 us (15%)
  between operations  17.1 us (10%)
  local copies, waits for them, and re-layouts  17 us (10%)
  blocking collectives  13.3 us (8%)
  waiting for transfers between devices  12.8 us (8%)
  starting transfers between devices  8.17 us (5%)
    sub x1, matrix products, local(): weights = jnp.exp(scores - jnp.max(scores, -1, keepdims=True))  19.3 us
    dot_general x1, matrix products, local(): jnp.einsum('hqk,khe->qhe', probs, all_values, preferred_element_type=jnp....  14.9 us
    dot_general x1, matrix products, local(): jnp.dot(img_full, w_img_qkv, preferred_element_type=jnp.float32)  14.3 us
    all_gather x1, blocking collectives, local(): lax.all_gather(latents.astype(jnp.bfloat16), 'mp', axis=0, tiled=True)  13.3 us
    all_to_all x1, waiting for transfers between devices, local(): mixed = lax.all_to_all(mixed, 'mp', split_axis=0, concat_axis=1, tiled=True)  12.5 us
    reduce_sum x3, other arithmetic, layer_norm(): spread = jnp.mean(center * center, -1, keepdims=True)  7.98 us
    dot_general x1, matrix products, local(): jnp.dot(txt_full, w_txt_kv, preferred_element_type=jnp.float32)  7.3 us
    dot_general x1, matrix products, local(): x_full = jnp.dot(lat_full, w_img_in, preferred_element_type=jnp.float32)  6.4 us
  transfers between devices with their start and end apart: 5, of which 2 were waited for; matrix products, arithmetic and copies ran while one was open for 38% of the time, Pallas kernels for 0%

profile of v1, /device:TPU:0, one launch (start us, length us, event | category | flops | bytes accessed | tf_op | source)
XLA Modules:
  0.0 161.9 jit_solution(1764503549173147141)
XLA Ops:
  7.2 1.3 dynamic_slice.48
  9.8 1.3 convert_reduce_fusion
  11.2 1.5 fusion.21
  13.3 1.5 dynamic-slice_add_fusion
  14.8 2.4 %fusion.24 = bf16[128,3072]{1,0:T(8,128)(2,1)} fusion(bf16[1,128,3072]{2,1,0:T(8,128)(2,1)} %param.19, f32[3072]{0:T(1024)S(1)} %bitcast.102, f32[3072]{0:T(1024)S(1)} %bitcast.103, f32[128]{0:T(128)S(1)} %add_rsqrt_fusion.5, f32[128]{0:T(128)S(1)} %broadcast_multiply_fusion.2), kind=kLoop, calls=%fused_computation.35 | loop fusion | flops 2359296 | bytes 1598464 | tf_op jit(solution)/shard_map/convert_element_type | solution.py:69
  17.9 13.3 %all_gather.7 = bf16[1024,64]{0,1:T(8,128)(2,1)S(1)} all-gather(bf16[256,64]{0,1:T(8,128)(2,1)S(1)} %convert_element_type.51), channel_id=1, replica_groups=mesh['cfg'=2,'group'=16,'mp'=4] {'mp'}, dimensions={0}, use_global_device_ids=true | all-gather | bytes 163840 | tf_op jit(solution)/shard_map/all_gather | solution.py:64
  31.1 6.4 %fusion.52 = (f32[1024]{0:T(1024)S(1)}, f32[1024,3072]{1,0:T(8,128)}) fusion(bf16[1024,64]{0,1:T(8,128)(2,1)S(1)} %all_gather.7, bf16[64,3072]{1,0:T(8,128)(2,1)S(1)} %copy-done), kind=kOutput, calls=%fused_computation.95 | convolution fusion | flops 405797888 | bytes 13111296 | tf_op jit(solution)/shard_map/dot_general | solution.py:65
  37.5 6.0 %multiply_reduce_fusion = f32[1024]{0:T(1024)S(1)} fusion(f32[1024,3072]{1,0:T(8,128)} %get-tuple-element.15, f32[1024]{0:T(1024)S(1)} %broadcast_multiply_fusion), kind=kLoop, calls=%fused_computation.10 | loop fusion | flops 9436160 | bytes 12591104 | tf_op jit(solution)/shard_map/reduce_sum | solution.py:17
  45.5 14.3 %fusion.6 = f32[1024,1152]{0,1:T(8,128)S(1)} fusion(bf16[3072,1152]{1,0:T(8,128)(2,1)} %param.21, f32[1024,3072]{1,0:T(8,128)} %get-tuple-element.15, f32[3072]{0:T(1024)S(1)} %bitcast.108, f32[3072]{0:T(1024)S(1)} %bitcast.107, f32[1024]{0:T(1024)S(1)} %add_rsqrt_fusion.3, f32[1024]{0:T(1024)S(1)} %broadcast_multiply_fusion), kind=kOutput, calls=%fused_computation.11 | convolution fusion | flops 7263485952 | bytes 24412160 | tf_op jit(solution)/shard_map/dot_general | solution.py:71
  59.7 2.1 %copy-done.1 = f32[1024,1152]{0,1:T(8,128)} copy-done((f32[1024,1152]{0,1:T(8,128)}, f32[1024,1152]{0,1:T(8,128)S(1)}, u32[]{:S(2)}) %copy-start.1) | copy-done | bytes 4718616
  62.6 1.4 fusion.50
  66.4 1.1 fusion.27
  67.6 7.3 %fusion.56 = f32[512,768]{1,0:T(8,128)} fusion(bf16[512,3072]{1,0:T(8,128)(2,1)} %all-gather.2.cloned.1.call-done, bf16[3072,768]{1,0:T(8,128)(2,1)} %param.22), kind=kOutput, calls=%fused_computation.99 | convolution fusion | flops 2415919104 | bytes 9437184 | tf_op jit(solution)/shard_map/dot_general | solution.py:77
  74.9 2.1 %reshape.127 = f32[512,3,2,128]{3,2,1,0:T(2,128)S(1)} reshape(f32[512,768]{1,0:T(8,128)} %fusion.56) | data formatting | bytes 3145728 | tf_op jit(solution)/shard_map/reshape | solution.py:77
  78.2 1.1 pad_maximum_fusion.2
  81.3 1.6 multiply_reduce_fusion.2
  83.5 1.5 fusion.36
  87.5 19.3 %fusion.53 = (f32[3,1024]{1,0:T(4,128)S(1)}, f32[3,1024,3072]{2,1,0:T(8,128)}) fusion(pred[3072]{0:T(1024)(128)(4,1)S(1)} %pad_add_fusion, bf16[1536,3,128]{2,0,1:T(8,128)(2,1)} %collective-permute-done.1, bf16[1024,3,128]{2,0,1:T(8,128)(2,1)} %copy-done.2, bf16[512,3,128]{2,0,1:T(8,128)(2,1)} %copy-done.3, f32[1024,3,3,128]{0,3,2,1:T(8,128)} %bitcast.99, ...), kind=kOutput, calls=%fused_computation.96 | convolution fusion | flops 2461928448 | bytes 41713152 | tf_op jit(solution)/shard_map/sub | solution.py:101
  106.8 14.9 %fusion.32 = bf16[1024,3,128]{0,2,1:T(8,128)(2,1)S(1)} fusion(f32[3,1024,3072]{2,1,0:T(8,128)} %get-tuple-element.17, f32[3,1024]{1,0:T(4,128)S(1)} %get-tuple-element.16, bf16[1536,3,128]{0,2,1:T(8,128)(2,1)} %collective-permute-done, bf16[1024,3,128]{0,2,1:T(8,128)(2,1)S(1)} %fusion.36, bf16[512,3,128]{0,2,1:T(8,128)(2,1)S(1)} %bitcast.101), kind=kOutput, calls=%fused_computation.47 | convolution fusion | flops 2442264576 | bytes 40906752 | tf_op jit(solution)/shard_map/hqk,khe->qhe/dot_general | solution.py:103
  123.2 4.3 %all-to-all-start = ((bf16[4,256,384]{1,2,0:T(8,128)(2,1)}), bf16[4,256,384]{1,2,0:T(8,128)(2,1)S(1)}, u32[]{:S(2)}, u32[]{:S(2)}) async-start(bf16[4,256,384]{1,2,0:T(8,128)(2,1)} %copy.33), calls=%async_computation | async-start | bytes 1572864 | tf_op jit(solution)/shard_map/all_to_all | solution.py:107
  127.5 12.5 %all-to-all-done = bf16[4,256,384]{1,2,0:T(8,128)(2,1)S(1)} async-done(((bf16[4,256,384]{1,2,0:T(8,128)(2,1)}), bf16[4,256,384]{1,2,0:T(8,128)(2,1)S(1)}, u32[]{:S(2)}, u32[]{:S(2)}) %all-to-all-start) | async-done | bytes 786464 | tf_op jit(solution)/shard_map/all_to_all | solution.py:107
  140.0 5.2 %convolution_multiply_fusion = f32[256,3072]{1,0:T(8,128)S(1)} fusion(bf16[256,1536]{0,1:T(8,128)(2,1)S(1)} %bitcast.95, bf16[1536,3072]{1,0:T(8,128)(2,1)} %param.25, f32[3072]{0:T(1024)S(1)} %bitcast.104), kind=kOutput, calls=%fused_computation.18 | convolution fusion | flops 2416705536 | bytes 13381632 | tf_op jit(solution)/shard_map/dot_general | solution.py:108
  147.7 3.3 %collective-permute-start.2 = (bf16[256,64]{0,1:T(8,128)(2,1)S(1)}, bf16[256,64]{0,1:T(8,128)(2,1)S(1)}, u32[]{:S(2)}, u32[]{:S(2)}) collective-permute-start(bf16[256,64]{0,1:T(8,128)(2,1)S(1)} %get-tuple-element.20), channel_id=1, source_target_pairs={{0,64},{64,0},{1,65},{65,1},{2,66},{66,2},{3,67},{67,3},{4,68},{68... | collective-permute-start | bytes 98312 | tf_op jit(solution)/shard_map/ppermute | solution.py:12
  153.2 1.9 %subtract_bitcast_fusion = (f32[1,128,64]{1,2,0:T(8,128)}, f32[1,128,64]{1,2,0:T(8,128)}) fusion(f32[256,64]{0,1:T(8,128)S(1)} %copy-done.7, s32[]{:T(128)S(6)} %select_n.65, f32[]{:T(128)} %bitcast.25, f32[]{:T(128)} %bitcast.23, f32[256,64]{0,1:T(8,128)S(1)} %get-tuple-element.21, bf16[256,64]{0,1:T(8,128)(2,1)S(1)} %collective-permute-done.2, pred[]{:T(512)S(6)} %eq.9, ...), kind=kLoop, calls=%fused_computation.62 | loop fusion | flops 73728 | bytes 147597 | tf_op jit(solution)/shard_map/broadcast_in_dim | solution.py:126
  (75 shorter events, 17.3 us)
Async XLA Ops:
  7.2 24.0 %copy-start = (bf16[64,3072]{1,0:T(8,128)(2,1)S(1)}, bf16[64,3072]{1,0:T(8,128)(2,1)}, u32[]{:S(2)}) copy-start(bf16[64,3072]{1,0:T(8,128)(2,1)} %param.20) | copy-start | bytes 1179652
  7.2 10.0 %copy-start.6 = (f32[256,64]{0,1:T(8,128)S(1)}, f32[256,64]{0,1:T(8,128)}, u32[]{:S(2)}) copy-start(f32[256,64]{0,1:T(8,128)} %param.18) | copy-start | bytes 196612
  7.2 60.4 %all-gather.2.cloned.1.call-start = ((), (), s32[]{:S(2)}) async-start(), calls=%async_computation.1 | async-start | bytes 3932160 | tf_op jit(solution)/shard_map/all_gather | solution.py:70
  17.2 0.6 copy-start.4
  59.7 2.2 %copy-start.1 = (f32[1024,1152]{0,1:T(8,128)}, f32[1024,1152]{0,1:T(8,128)S(1)}, u32[]{:S(2)}) copy-start(f32[1024,1152]{0,1:T(8,128)S(1)} %fusion.6) | copy-start | bytes 14155780
  61.9 0.7 copy-start.10
  67.6 10.6 %copy-start.2 = (bf16[1024,3,128]{2,0,1:T(8,128)(2,1)}, bf16[1024,3,128]{2,0,1:T(8,128)(2,1)S(1)}, u32[]{:S(2)}) copy-start(bf16[1024,3,128]{2,0,1:T(8,128)(2,1)S(1)} %fusion.27) | copy-start | bytes 2359300
  74.9 3.0 %copy-start.11 = (f32[128]{0:T(128)S(1)}, f32[128]{0:T(128)}, u32[]{:S(2)}) copy-start(f32[128]{0:T(128)} %param.24) | copy-start | bytes 1540
  77.0 3.0 %copy-start.12 = (s32[2,16]{1,0:T(2,128)S(1)}, s32[2,16]{1,0:T(2,128)}, u32[]{:S(2)}) copy-start(s32[2,16]{1,0:T(2,128)} %param.34) | copy-start | bytes 388
  78.2 1.2 copy-start.3
  79.3 8.2 %collective-permute-start.1 = (bf16[1536,3,128]{2,0,1:T(8,128)(2,1)}, bf16[1536,3,128]{2,0,1:T(8,128)(2,1)}, u32[]{:S(2)}, u32[]{:S(2)}) collective-permute-start(bf16[1536,3,128]{2,0,1:T(8,128)(2,1)} %pad_maximum_fusion.2), channel_id=1, source_target_pairs={{0,4},{4,0},{8,12},{12,8},{16,20},{20,16},{24,28},{28,24},{32,36},... | collective-permute-start | bytes 3538952 | tf_op jit(solution)/shard_map/ppermute | solution.py:12
  86.9 19.9 %collective-permute-start = (bf16[1536,3,128]{0,2,1:T(8,128)(2,1)S(1)}, bf16[1536,3,128]{0,2,1:T(8,128)(2,1)}, u32[]{:S(2)}, u32[]{:S(2)}) collective-permute-start(bf16[1536,3,128]{0,2,1:T(8,128)(2,1)S(1)} %pad_maximum_fusion.1), channel_id=1, source_target_pairs={{0,4},{4,0},{8,12},{12,8},{16,20},{20,16},{24,28},{28,24},{32,36},... | collective-permute-start | bytes 3538952 | tf_op jit(solution)/shard_map/ppermute | solution.py:12
  123.2 16.7 %all-to-all-start = ((bf16[4,256,384]{1,2,0:T(8,128)(2,1)}), bf16[4,256,384]{1,2,0:T(8,128)(2,1)S(1)}, u32[]{:S(2)}, u32[]{:S(2)}) async-start(bf16[4,256,384]{1,2,0:T(8,128)(2,1)} %copy.33), calls=%async_computation | async-start | bytes 1572864 | tf_op jit(solution)/shard_map/all_to_all | solution.py:107
  140.0 5.2 %copy-start.5 = (bf16[256,64]{0,1:T(8,128)(2,1)S(1)}, bf16[256,64]{0,1:T(8,128)(2,1)}, u32[]{:S(2)}) copy-start(bf16[256,64]{0,1:T(8,128)(2,1)} %copy-done.4) | copy-start | bytes 98308
  145.9 0.7 copy-start.8
  145.9 0.7 copy-start.9
  145.9 1.0 copy-start.13
  145.9 5.7 %copy-start.14 = (f32[8]{0:T(128)S(1)}, f32[8]{0:T(128)}, u32[]{:S(2)}) copy-start(f32[8]{0:T(128)} %param.31) | copy-start | bytes 100
  145.9 6.4 %copy-start.15 = (f32[16]{0:T(128)S(1)}, f32[16]{0:T(128)}, u32[]{:S(2)}) copy-start(f32[16]{0:T(128)} %param.30) | copy-start | bytes 196
  145.9 7.2 %copy-start.7 = (f32[256,64]{0,1:T(8,128)S(1)}, f32[256,64]{0,1:T(8,128)}, u32[]{:S(2)}) copy-start(f32[256,64]{0,1:T(8,128)} %param.18) | copy-start | bytes 196612
  147.7 5.5 %collective-permute-start.2 = (bf16[256,64]{0,1:T(8,128)(2,1)S(1)}, bf16[256,64]{0,1:T(8,128)(2,1)S(1)}, u32[]{:S(2)}, u32[]{:S(2)}) collective-permute-start(bf16[256,64]{0,1:T(8,128)(2,1)S(1)} %get-tuple-element.20), channel_id=1, source_target_pairs={{0,64},{64,0},{1,65},{65,1},{2,66},{66,2},{3,67},{67,3},{4,68},{68... | collective-permute-start | bytes 98312 | tf_op jit(solution)/shard_map/ppermute | solution.py:12
Sparse Core Ops, SparseCore 0:
  17.3 42.2 all-gather.1

commit v2 on v1

v2 whole, which is shorter than its diff:
```python
import functools
import math

import jax
import jax.numpy as jnp
from jax import lax
from jax.experimental import pallas as pl
from jax.experimental.pallas import tpu as pltpu
from jax.sharding import PartitionSpec as P

HD = 128
F32 = jnp.float32
BF16 = jnp.bfloat16
MESH = pl.DeviceIdType.MESH
TEXT_FROM = (0, 1, 3, 2)


def nt_dot(a, b):
    return lax.dot_general(a, b, (((1,), (1,)), ((), ())), preferred_element_type=F32)


def dot(a, b):
    return jnp.dot(a, b, preferred_element_type=F32)


def head_norm(values, gain):
    return values * lax.rsqrt(jnp.mean(values * values, -1, keepdims=True) + 1e-06) * gain


def split(values):
    high = values.astype(BF16)
    return high, (values - high.astype(F32)).astype(BF16)


def body(
    lat_h, text_h, win_h, wq_h, wt_h, wo_h, wf_h, mimg_h, mtxt_h, mfin_h,
    qg, kg, guide, step_size, img_len, txt_len, flags, tstep,
    vel_o, next_o,
    lat, text, win, wq, wt, wo, wf, mimg, mtxt, mfin,
    txt, lall, wx, lhs, rhs, bias, xc, q, kv, kvm, mask, maskm, acc, att,
    mix, mixr, relay, fin, vsend, vrecv,
    lsem, ts, tr, ls, lr, ks, kr, ms, mr, vs, vr,
):
    c = lax.axis_index("cfg")
    g = lax.axis_index("group")
    m = lax.axis_index("mp")
    n_mp = 4
    right, left = lax.rem(m + 1, n_mp), lax.rem(m + 3, n_mp)
    mate = g + 1 - 2 * lax.rem(g, 2)
    rows, ch = lat_h.shape
    trows, d = text_h.shape
    heads = wq_h.shape[1] // (3 * HD)
    img, ntxt = rows * n_mp, trows * n_mp
    half = rows // 2
    part = trows // 4

    def local_copy(src, dst, i):
        copy = pltpu.make_async_copy(src, dst, lsem.at[i])
        copy.start()
        return copy

    c_text = local_copy(text_h, text, 0)
    c_mtxt = local_copy(mtxt_h, mtxt, 1)
    c_lat = local_copy(lat_h, lat, 2)
    c_win = local_copy(win_h, win, 3)
    c_mimg = local_copy(mimg_h, mimg, 4)
    c_wq = [
        local_copy(wq_h.at[:, pl.ds(h * 3 * HD, 3 * HD)], wq.at[h], 5 + h) for h in range(heads)
    ]
    c_wt = local_copy(wt_h, wt, 5 + heads)
    c_wo = local_copy(wo_h, wo, 6 + heads)
    c_wf = local_copy(wf_h, wf, 7 + heads)
    c_mfin = local_copy(mfin_h, mfin, 8 + heads)

    barrier = pltpu.get_barrier_semaphore()
    for k in (1, 2, 3):
        pl.semaphore_signal(
            barrier, inc=1, device_id={"mp": lax.rem(m + k, n_mp)}, device_id_type=MESH
        )
    pl.semaphore_signal(barrier, inc=1, device_id={"group": mate}, device_id_type=MESH)
    pl.semaphore_signal(barrier, inc=1, device_id={"cfg": 1 - c}, device_id_type=MESH)

    def remote(src, dst, ssem, rsem, device):
        return pltpu.make_async_remote_copy(
            src_ref=src, dst_ref=dst, send_sem=ssem, recv_sem=rsem,
            device_id=device, device_id_type=MESH,
        )

    step = tstep[g]
    il, tl = img_len[g], txt_len[g]
    il_m, tl_m = img_len[mate], txt_len[mate]
    flag = jnp.where(flags[c, g] == 1, 1.0, 0.0).astype(F32)

    def chunk(i):
        return pl.ds(i * part, part)

    to_right = [
        remote(txt.at[0, chunk(i)], txt.at[2, chunk(i)], ts.at[i], tr.at[i], {"mp": right})
        for i in range(4)
    ]
    to_left = [
        remote(txt.at[0, chunk(i)], txt.at[1, chunk(i)], ts.at[4 + i], tr.at[4 + i], {"mp": left})
        for i in range(4)
    ]
    on_right = [
        remote(txt.at[2, chunk(i)], txt.at[3, chunk(i)], ts.at[8 + i], tr.at[8 + i], {"mp": right})
        for i in (0, 1)
    ]
    on_left = [
        remote(txt.at[1, chunk(i)], txt.at[3, chunk(i)], ts.at[8 + i], tr.at[8 + i], {"mp": left})
        for i in (2, 3)
    ]

    def norm_text(i):
        x = text[chunk(i), :].astype(F32)
        center = x - jnp.mean(x, -1, keepdims=True)
        spread = jnp.mean(center * center, -1, keepdims=True)
        y = center * lax.rsqrt(spread + 1e-06) * (1.0 + mtxt[step, 1:2, :]) + mtxt[step, 0:1, :]
        txt[0, chunk(i), :] = y.astype(BF16)

    c_text.wait()
    c_mtxt.wait()
    norm_text(0)
    norm_text(2)
    pl.semaphore_wait(barrier, 5)
    to_right[0].start()
    to_left[2].start()

    c_lat.wait()
    c_win.wait()
    c_mimg.wait()
    e_row = lax.broadcasted_iota(jnp.int32, (ch, 2 * ch), 0)
    e_col = lax.broadcasted_iota(jnp.int32, (ch, 2 * ch), 1)
    twice = jnp.where((e_col == e_row) | (e_col == e_row + ch), 1.0, 0.0).astype(BF16)
    lat2 = dot(lat[...].astype(BF16), twice)
    w = win[...].astype(F32)
    w = w - jnp.mean(w, -1, keepdims=True)
    w_high, w_low = split(w)
    wx[0:ch, :] = w_high
    wx[ch : 2 * ch, :] = w_low
    s_high, s_low = split(w * (1.0 + mimg[step, 1:2, :]))
    lhs[0:ch, :] = s_high
    lhs[ch : 2 * ch, :] = s_low
    b_high, b_low = split(mimg[step, 0:1, :])
    b_row = lax.broadcasted_iota(jnp.int32, (16, d), 0)
    lhs[2 * ch :, :] = jnp.where(
        b_row == 0, b_high.astype(F32), jnp.where(b_row == 1, b_low.astype(F32), 0.0)
    ).astype(BF16)
    lat2b = lat2.astype(BF16)
    squares = jnp.zeros((rows, HD), F32)
    wide = min(d, 512)
    for j in range(d // wide):
        x = dot(lat2b, wx[:, j * wide : (j + 1) * wide])
        xc[:, j * wide : (j + 1) * wide] = x
        for k in range(wide // HD):
            piece = x[:, k * HD : (k + 1) * HD]
            squares = squares + piece * piece
    rstd = lax.rsqrt(jnp.sum(squares, -1, keepdims=True) / d + 1e-06)
    scaled = lat2 * rstd
    scaled_high = scaled.astype(BF16).astype(F32)
    lane = lax.broadcasted_iota(jnp.int32, (rows, 2 * ch), 1)
    lall[0] = jnp.where(lane < ch, scaled_high, scaled - scaled_high).astype(BF16)
    lat_out = [
        remote(
            lall.at[0], lall.at[4 - k], ls.at[k - 1], lr.at[k - 1], {"mp": lax.rem(m + k, n_mp)}
        )
        for k in (1, 2, 3)
    ]
    for copy in lat_out:
        copy.start()

    norm_text(1)
    norm_text(3)
    to_right[1].start()
    to_left[3].start()
    to_right[2].start()
    to_left[0].start()
    to_right[3].start()
    to_left[1].start()

    def fill_mask(ref, img_live, txt_live):
        spot = lax.broadcasted_iota(jnp.int32, (rows, HD), 0)
        for k in range(4):
            start = lax.rem(m + k, n_mp) * rows
            ref[k * rows : (k + 1) * rows, :] = jnp.where(
                spot + start < img_live, 1.0, 0.0
            ).astype(BF16)
        spot_t = lax.broadcasted_iota(jnp.int32, (trows, HD), 0)
        for k in range(4):
            start = lax.rem(m + TEXT_FROM[k], n_mp) * trows
            ref[img + k * trows : img + (k + 1) * trows, :] = jnp.where(
                spot_t + start < txt_live, 1.0, 0.0
            ).astype(BF16)

    fill_mask(mask, il, tl)
    fill_mask(maskm, il_m, tl_m)

    for h in range(heads):
        c_wq[h].wait()
        full = dot(lhs[...], wq[h])
        fold = full[0:ch] + full[ch : 2 * ch]
        high, low = split(fold)
        rhs[h, 0:ch, :] = high
        rhs[h, ch : 2 * ch, :] = high
        rhs[h, 2 * ch : 3 * ch, :] = low
        rhs[h, 3 * ch : 4 * ch, :] = low
        bias[h] = full[2 * ch : 2 * ch + 8]
    for copy in lat_out:
        copy.wait_recv()
    q_gain = qg[...] * (HD ** (-0.5) * math.log2(math.e))
    k_gain = kg[...]
    kv_img = []
    for h in range(heads):

        def image_block(k, carry, h=h):
            block = lall[k]
            at = pl.ds(pl.multiple_of(k * rows, rows), rows)
            both = bias[h, 0:1, :] + bias[h, 1:2, :]
            x = dot(jnp.concatenate([block, block], axis=1), rhs[h]) + both
            q[h, at, :] = head_norm(x[:, 0:HD], q_gain).astype(BF16)
            kv[h, at, 0:HD] = head_norm(x[:, HD : 2 * HD], k_gain).astype(BF16)
            kv[h, at, HD : 2 * HD] = x[:, 2 * HD :].astype(BF16) * mask[at, :]
            return carry

        lax.fori_loop(0, n_mp, image_block, 0)
        copy = remote(
            kv.at[h, pl.ds(0, img)], kvm.at[h, pl.ds(0, img)], ks.at[h], kr.at[h],
            {"group": mate},
        )
        copy.start()
        kv_img.append(copy)

    def text_block(first, count):
        span = slice(img + first * trows, img + (first + count) * trows)
        lhs_t = txt[first] if count == 1 else jnp.concatenate(
            [txt[first + k] for k in range(count)], axis=0
        )
        for h in range(heads):
            x = dot(lhs_t, wt[:, h * 2 * HD : (h + 1) * 2 * HD])
            kv[h, span, 0:HD] = head_norm(x[:, 0:HD], k_gain).astype(BF16)
            kv[h, span, HD : 2 * HD] = x[:, HD:].astype(BF16) * mask[span, :]
        i = heads + first if first < 2 else heads + 2
        copy = remote(
            kv.at[:, pl.ds(img + first * trows, count * trows)],
            kvm.at[:, pl.ds(img + first * trows, count * trows)],
            ks.at[i], kr.at[i], {"group": mate},
        )
        copy.start()
        return copy

    c_wt.wait()
    kv_txt = [text_block(0, 1)]

    def attend(ref, mref, h, at, lo, n):
        s = nt_dot(q[h, at, :], ref[h, lo : lo + n, 0:HD])
        p = jnp.exp2(s).astype(BF16)
        return dot(
            p, jnp.concatenate([ref[h, lo : lo + n, HD : 2 * HD], mref[lo : lo + n, :]], axis=1)
        )

    def each_block(fn):
        def run(i, carry):
            h, k = i // n_mp, lax.rem(i, n_mp)
            fn(h, pl.ds(pl.multiple_of(k * rows, rows), rows))
            return carry

        lax.fori_loop(0, heads * n_mp, run, 0)

    def own_image(h, at):
        acc[h, at, :] = attend(kv, mask, h, at, 0, img)

    each_block(own_image)

    to_right[0].wait_recv()
    on_right[0].start()
    to_left[2].wait_recv()
    on_left[0].start()
    for copy in kv_img:
        copy.wait_recv()

    def mate_image(h, at):
        acc[h, at, :] += flag * attend(kvm, maskm, h, at, 0, img)

    each_block(mate_image)

    to_right[1].wait_recv()
    on_right[1].start()
    to_left[3].wait_recv()
    on_left[1].start()
    to_right[2].wait_recv()
    to_right[3].wait_recv()
    to_left[0].wait_recv()
    to_left[1].wait_recv()
    kv_txt.append(text_block(1, 2))
    kv_txt[0].wait_recv()
    kv_txt[1].wait_recv()

    def most_text(h, at):
        own = attend(kv, mask, h, at, img, 3 * trows)
        other = attend(kvm, maskm, h, at, img, 3 * trows)
        acc[h, at, :] += own + flag * other

    each_block(most_text)

    for copy in on_right + on_left:
        copy.wait_recv()
    kv_txt.append(text_block(3, 1))
    last = img + 3 * trows

    kv_txt[2].wait_recv()

    def last_block(k):
        at = slice(k * rows, (k + 1) * rows)

        def run(h, carry):
            own = attend(kv, mask, h, at, last, trows)
            other = attend(kvm, maskm, h, at, last, trows)
            total = acc[h, at, :] + own + flag * other
            mix[k, h] = (total[:, 0:HD] / total[:, HD : 2 * HD]).astype(BF16)
            return carry

        lax.fori_loop(0, heads, run, 0)

    first_half, second_half = pl.ds(0, half), pl.ds(half, half)
    hop_a = remote(mix.at[2, :, first_half], relay.at[0], ms.at[0], mr.at[0], {"mp": right})
    hop_b = remote(mix.at[2, :, second_half], relay.at[1], ms.at[1], mr.at[1], {"mp": left})
    mix_r = remote(mix.at[1], mixr.at[2], ms.at[2], mr.at[2], {"mp": right})
    mix_l = remote(mix.at[3], mixr.at[0], ms.at[3], mr.at[3], {"mp": left})
    fwd_a = remote(relay.at[0], mixr.at[1, :, first_half], ms.at[4], mr.at[4], {"mp": right})
    fwd_b = remote(relay.at[1], mixr.at[1, :, second_half], ms.at[5], mr.at[5], {"mp": left})

    last_block(2)
    hop_a.start()
    hop_b.start()
    last_block(1)
    mix_r.start()
    last_block(3)
    mix_l.start()
    last_block(0)
    hop_a.wait_recv()
    fwd_a.start()
    hop_b.wait_recv()
    fwd_b.start()
    c_wo.wait()

    def project(ref, k, first):
        base = pl.multiple_of(lax.rem(m + k, n_mp) * (heads * HD), heads * HD)
        own = jnp.concatenate([ref[h] for h in range(heads)], axis=1)
        for j in range(d // wide):
            cols = slice(j * wide, (j + 1) * wide)
            x = dot(own, wo[pl.ds(base, heads * HD), cols])
            att[:, cols] = x if first else att[:, cols] + x

    project(mix.at[0], 0, True)
    mix_r.wait_recv()
    project(mixr.at[2], 3, False)
    mix_l.wait_recv()
    project(mixr.at[0], 1, False)
    fwd_a.wait_recv()
    fwd_b.wait_recv()
    project(mixr.at[1], 2, False)
    c_wf.wait()
    c_mfin.wait()

    def finish(start):
        small = min(half, 32)

        def run(i, carry):
            at = pl.ds(pl.multiple_of(start + i * small, small), small)
            x = xc[at, :] + mimg[step, 2:3, :] * att[at, :]
            center = x - jnp.mean(x, -1, keepdims=True)
            spread = jnp.mean(center * center, -1, keepdims=True)
            y = center * lax.rsqrt(spread + 1e-06) * (1.0 + mfin[step, 1:2, :]) + mfin[step, 0:1, :]
            fin[pl.ds(pl.multiple_of(i * small, small), small), :] = y.astype(BF16)
            return carry

        lax.fori_loop(0, half // small, run, 0)
        return dot(fin[...], wf[...])

    vsend[...] = finish(pl.multiple_of((1 - c) * half, half))
    swap = remote(vsend, vrecv, vs.at[0], vr.at[0], {"cfg": 1 - c})
    swap.start()
    own = finish(pl.multiple_of(c * half, half))
    swap.wait_recv()
    other = vrecv[...]
    cond = jnp.where(c == 0, own, other)
    uncond = jnp.where(c == 0, other, own)
    guided = uncond + guide[g] * (cond - uncond)
    spot = lax.broadcasted_iota(jnp.int32, (half, ch), 0) + (m * rows + c * half)
    guided = jnp.where(spot < il, guided, 0.0)
    vel_o[...] = guided
    next_o[...] = lat[pl.ds(pl.multiple_of(c * half, half), half), :] - step_size[step] * guided

    for copy in to_right + to_left + on_right + on_left + lat_out + kv_img + kv_txt:
        copy.wait_send()
    for copy in (hop_a, hop_b, mix_r, mix_l, fwd_a, fwd_b, swap):
        copy.wait_send()


def local(
    latents, text_hidden, w_img_in, w_img_qkv, w_txt_kv, q_gain, k_gain, w_out, w_final,
    mod_img, mod_txt, mod_final, guide, step_size, img_len, txt_len, split_flag, tstep,
):
    text = text_hidden[0]
    rows, ch = latents.shape
    trows, d = text.shape
    heads = w_img_qkv.shape[1] // (3 * HD)
    img, ntxt = 4 * rows, 4 * trows
    half = rows // 2
    hbm = pl.BlockSpec(memory_space=pl.ANY)
    vmem = pl.BlockSpec(memory_space=pltpu.VMEM)
    smem = pl.BlockSpec(memory_space=pltpu.SMEM)
    dma = pltpu.SemaphoreType.DMA
    out = jax.ShapeDtypeStruct((half, ch), F32)
    scratch = [
        pltpu.VMEM(latents.shape, F32),
        pltpu.VMEM(text.shape, BF16),
        pltpu.VMEM(w_img_in.shape, BF16),
        pltpu.VMEM((heads, d, 3 * HD), BF16),
        pltpu.VMEM(w_txt_kv.shape, BF16),
        pltpu.VMEM(w_out.shape, BF16),
        pltpu.VMEM(w_final.shape, BF16),
        pltpu.VMEM(mod_img.shape, F32),
        pltpu.VMEM(mod_txt.shape, F32),
        pltpu.VMEM(mod_final.shape, F32),
        pltpu.VMEM((4, trows, d), BF16),
        pltpu.VMEM((4, rows, 2 * ch), BF16),
        pltpu.VMEM((2 * ch, d), BF16),
        pltpu.VMEM((2 * ch + 16, d), BF16),
        pltpu.VMEM((heads, 4 * ch, 3 * HD), BF16),
        pltpu.VMEM((heads, 8, 3 * HD), F32),
        pltpu.VMEM((rows, d), F32),
        pltpu.VMEM((heads, img, HD), BF16),
        pltpu.VMEM((heads, img + ntxt, 2 * HD), BF16),
        pltpu.VMEM((heads, img + ntxt, 2 * HD), BF16),
        pltpu.VMEM((img + ntxt, HD), BF16),
        pltpu.VMEM((img + ntxt, HD), BF16),
        pltpu.VMEM((heads, img, 2 * HD), F32),
        pltpu.VMEM((rows, d), F32),
        pltpu.VMEM((4, heads, rows, HD), BF16),
        pltpu.VMEM((3, heads, rows, HD), BF16),
        pltpu.VMEM((2, heads, half, HD), BF16),
        pltpu.VMEM((half, d), BF16),
        pltpu.VMEM((half, ch), F32),
        pltpu.VMEM((half, ch), F32),
        dma((9 + heads,)),
        dma((12,)), dma((12,)),
        dma((3,)), dma((3,)),
        dma((heads + 3,)), dma((heads + 3,)),
        dma((6,)), dma((6,)),
        dma((1,)), dma((1,)),
    ]
    velocity, moved = pl.pallas_call(
        body,
        out_shape=(out, out),
        in_specs=[hbm] * 10 + [vmem] * 2 + [smem] * 6,
        out_specs=(vmem, vmem),
        scratch_shapes=scratch,
        compiler_params=pltpu.CompilerParams(
            collective_id=0, has_side_effects=True, vmem_limit_bytes=61 * 1024 * 1024
        ),
        name="guided_step",
    )(
        latents, text, w_img_in, w_img_qkv, w_txt_kv, w_out, w_final, mod_img, mod_txt, mod_final,
        q_gain[None], k_gain[None], guide, step_size, img_len, txt_len, split_flag, tstep,
    )
    return velocity[None], moved[None]


def solution(mesh):
    rep = P()
    placed = (
        P(("group", "mp"), None), P("cfg", ("group", "mp"), None), rep,
        P(None, "mp"), P(None, "mp"),
    ) + (rep,) * 13
    out = P("cfg", ("group", "mp"), None)
    return jax.shard_map(
        local, mesh=mesh, in_specs=placed, out_specs=(out, out), check_vma=False
    )
```

time: 163 us -> 75.2 us (0.46)
  matrix products: 68.8 us -> 0 us
  Pallas kernels: 0 us -> 65.4 us
  other arithmetic: 24.9 us -> 0 us
  between operations: 17.1 us -> 0.64 us
  blocking collectives: 13.3 us -> 0 us
  waiting for transfers between devices: 12.8 us -> 0 us
  local copies, waits for them, and re-layouts: 17 us -> 8.73 us
  starting transfers between devices: 8.17 us -> 0 us
    pallas_call x0 -> x1, Pallas kernels: none -> 65.4 us  [local(): pl.pallas_call(body, out_shape=(out, out), in_specs=[hbm] * 10 + [vmem] *...]
    dot_general x7 -> x0, matrix products: 49.4 us -> none  [the longest x1 14.9 us: local(): jnp.einsum('hqk,khe->qhe', probs, all_values, preferred_element_type=jnp....]
    sub x1 -> x0, matrix products: 19.3 us -> none  [local(): weights = jnp.exp(scores - jnp.max(scores, -1, keepdims=True))]
    all_gather x1 -> x0, blocking collectives: 13.3 us -> none  [local(): lax.all_gather(latents.astype(jnp.bfloat16), 'mp', axis=0, tiled=True)]
    all_to_all x1 -> x0, waiting for transfers between devices: 12.5 us -> none  [local(): mixed = lax.all_to_all(mixed, 'mp', split_axis=0, concat_axis=1, tiled=True)]
    reduce_sum x7 -> x0, other arithmetic: 11.6 us -> none  [the longest x3 7.98 us: layer_norm(): spread = jnp.mean(center * center, -1, keepdims=True)]
    dynamic_slice x5 -> x0, local copies, waits for them, and re-layouts: 4.53 us -> none  [pick_entry(): return lax.dynamic_index_in_dim(table, index, 0, keepdims=False)]
    all_to_all x1 -> x0, starting transfers between devices: 4.26 us -> none  [local(): mixed = lax.all_to_all(mixed, 'mp', split_axis=0, concat_axis=1, tiled=True)]
  transfers between devices with their start and end apart: 5 -> 0, of which waited for: 2 -> 0; matrix products, arithmetic and copies ran while one was open for 38% -> 0% of each run, Pallas kernels for 0% -> 0%
where the time goes in v2:
time: 75.2 us; the launch traced here: 74.8 us
  Pallas kernels  65.4 us (87%)
  local copies, waits for them, and re-layouts  8.73 us (12%)
    pallas_call x1, Pallas kernels, local(): pl.pallas_call(body, out_shape=(out, out), in_specs=[hbm] * 10 + [vmem] *...  65.4 us
    unnamed x5, local copies, waits for them, and re-layouts  8.73 us

profile of v2, /device:TPU:0, one launch (start us, length us, event | category | flops | bytes accessed | tf_op | source)
XLA Modules:
  0.0 74.8 jit_solution(7570751929825417739)
XLA Ops:
  0.6 1.6 %copy.20.lat_h = f32[256,64]{1,0:T(8,128)} copy(f32[256,64]{0,1:T(8,128)} %param.18) | data formatting | bytes 131072 | tf_op args[0]
  2.2 1.9 %copy.22.mimg_h = f32[8,3,3072]{2,1,0:T(4,128)} copy(f32[8,3,3072]{2,0,1:T(8,128)} %param.27) | data formatting | bytes 589824 | tf_op args[9]
  4.1 2.2 %copy.21.wf_h = bf16[3072,64]{1,0:T(8,128)(2,1)} copy(bf16[3072,64]{0,1:T(8,128)(2,1)} %param.26) | data formatting | bytes 786432 | tf_op args[8]
  6.3 65.4 %guided_step.1 = (f32[128,64]{1,0:T(8,128)}, f32[128,64]{1,0:T(8,128)}) custom-call(f32[256,64]{1,0:T(8,128)} %copy.20.lat_h, bf16[128,3072]{1,0:T(8,128)(2,1)} %bitcast.5, bf16[64,3072]{1,0:T(8,128)(2,1)} %win_h.1, bf16[3072,1152]{1,0:T(8,128)(2,1)} %wq_h.1, bf16[3072,768]{1,0:T(8,128)(2,1)} %wt_h.1, bf16[1536,3072]{1,0:T(8,128)(2,1)} %wo_h.1, ...), custom_call_target="tpu_custom_call" | custom-call | tf_op jit(solution)/shard_map/guided_step/pallas_call | solution.py:453
  71.7 1.5 %copy.23 = f32[1,128,64]{1,2,0:T(8,128)} copy(f32[1,128,64]{2,1,0:T(8,128)} %bitcast.7) | data formatting | bytes 65536
  73.3 1.5 %copy.24 = f32[1,128,64]{1,2,0:T(8,128)} copy(f32[1,128,64]{2,1,0:T(8,128)} %bitcast.6) | data formatting | bytes 65536

commit v3 on v2

v3 whole, which is shorter than its diff:
```python
import functools
import math

import jax
import jax.numpy as jnp
from jax import lax
from jax.experimental import pallas as pl
from jax.experimental.pallas import tpu as pltpu
from jax.sharding import PartitionSpec as P

HD = 128
F32 = jnp.float32
BF16 = jnp.bfloat16
MESH = pl.DeviceIdType.MESH
TEXT_FROM = (0, 1, 3, 2)


def nt_dot(a, b):
    return lax.dot_general(a, b, (((1,), (1,)), ((), ())), preferred_element_type=F32)


def dot(a, b):
    return jnp.dot(a, b, preferred_element_type=F32)


def head_norm(values, gain):
    return values * lax.rsqrt(jnp.mean(values * values, -1, keepdims=True) + 1e-06) * gain


def split(values):
    high = values.astype(BF16)
    return high, (values - high.astype(F32)).astype(BF16)


def body(
    lat_h, text_h, win_h, wq_h, wt_h, wo_h, wf_h, mimg_h, mtxt_h, mfin_h,
    qg, kg, guide, step_size, img_len, txt_len, flags, tstep,
    vel_o, next_o,
    lat, text, win, wq, wt, wo, wf, mimg, mtxt, mfin,
    txt, lall, wx, lhs, rhs, bias, xc, q, kv, kvm, mask, maskm, acc, att,
    mix, mixr, fin, vsend, vrecv,
    lsem, ts, tr, ls, lr, ks, kr, ms, mr, vs, vr,
):
    c = lax.axis_index("cfg")
    g = lax.axis_index("group")
    m = lax.axis_index("mp")
    n_mp = 4
    right, left = lax.rem(m + 1, n_mp), lax.rem(m + 3, n_mp)
    mate = g + 1 - 2 * lax.rem(g, 2)
    ch, rows = lat_h.shape
    trows, d = text_h.shape
    heads = wq_h.shape[1] // (3 * HD)
    img, ntxt = rows * n_mp, trows * n_mp
    half = rows // 2
    part = trows // 4

    def chunk(i):
        return pl.ds(i * part, part)

    def local_copy(src, dst, i):
        copy = pltpu.make_async_copy(src, dst, lsem.at[i])
        copy.start()
        return copy

    c_text = {
        i: local_copy(text_h.at[chunk(i)], text.at[chunk(i)], 9 + heads + i) for i in (0, 2)
    }
    c_mtxt = local_copy(mtxt_h, mtxt, 1)
    c_lat = local_copy(lat_h, lat, 2)
    c_win = local_copy(win_h, win, 3)
    c_mimg = local_copy(mimg_h, mimg, 4)
    for i in (1, 3):
        c_text[i] = local_copy(text_h.at[chunk(i)], text.at[chunk(i)], 9 + heads + i)

    barrier = pltpu.get_barrier_semaphore()
    for k in (1, 2, 3):
        pl.semaphore_signal(
            barrier, inc=1, device_id={"mp": lax.rem(m + k, n_mp)}, device_id_type=MESH
        )
    pl.semaphore_signal(barrier, inc=1, device_id={"group": mate}, device_id_type=MESH)
    pl.semaphore_signal(barrier, inc=1, device_id={"cfg": 1 - c}, device_id_type=MESH)

    def remote(src, dst, ssem, rsem, device):
        return pltpu.make_async_remote_copy(
            src_ref=src, dst_ref=dst, send_sem=ssem, recv_sem=rsem,
            device_id=device, device_id_type=MESH,
        )

    step = tstep[g]
    il, tl = img_len[g], txt_len[g]
    il_m, tl_m = img_len[mate], txt_len[mate]
    flag = jnp.where(flags[c, g] == 1, 1.0, 0.0).astype(F32)

    to_right = [
        remote(txt.at[0, chunk(i)], txt.at[2, chunk(i)], ts.at[i], tr.at[i], {"mp": right})
        for i in range(4)
    ]
    to_left = [
        remote(txt.at[0, chunk(i)], txt.at[1, chunk(i)], ts.at[4 + i], tr.at[4 + i], {"mp": left})
        for i in range(4)
    ]
    on_right = [
        remote(txt.at[2, chunk(i)], txt.at[3, chunk(i)], ts.at[8 + i], tr.at[8 + i], {"mp": right})
        for i in (0, 1)
    ]
    on_left = [
        remote(txt.at[1, chunk(i)], txt.at[3, chunk(i)], ts.at[8 + i], tr.at[8 + i], {"mp": left})
        for i in (2, 3)
    ]

    def norm_text(i):
        x = text[chunk(i), :].astype(F32)
        center = x - jnp.mean(x, -1, keepdims=True)
        spread = jnp.mean(center * center, -1, keepdims=True)
        y = center * lax.rsqrt(spread + 1e-06) * (1.0 + mtxt[step, 1:2, :]) + mtxt[step, 0:1, :]
        txt[0, chunk(i), :] = y.astype(BF16)

    c_mtxt.wait()
    c_text[0].wait()
    norm_text(0)
    c_text[2].wait()
    norm_text(2)
    pl.semaphore_wait(barrier, 5)
    to_right[0].start()
    to_left[2].start()
    c_lat.wait()
    c_win.wait()
    c_mimg.wait()
    c_wq = [
        local_copy(wq_h.at[:, pl.ds(h * 3 * HD, 3 * HD)], wq.at[h], 5 + h) for h in range(heads)
    ]
    c_wt = local_copy(wt_h, wt, 5 + heads)

    e_row = lax.broadcasted_iota(jnp.int32, (ch, 2 * ch), 0)
    e_col = lax.broadcasted_iota(jnp.int32, (ch, 2 * ch), 1)
    twice = jnp.where((e_col == e_row) | (e_col == e_row + ch), 1.0, 0.0).astype(BF16)
    lat2 = lax.dot_general(
        lat[...].astype(BF16), twice, (((0,), (0,)), ((), ())), preferred_element_type=F32
    )
    w = win[...].astype(F32)
    w = w - jnp.mean(w, -1, keepdims=True)
    w_high, w_low = split(w)
    wx[0:ch, :] = w_high
    wx[ch : 2 * ch, :] = w_low
    lat2b = lat2.astype(BF16)
    squares = jnp.zeros((rows, HD), F32)
    wide = min(d, 512)
    for j in range(d // wide):
        x = dot(lat2b, wx[:, j * wide : (j + 1) * wide])
        xc[1 - c, :, j * wide : (j + 1) * wide] = x[0:half]
        xc[c, :, j * wide : (j + 1) * wide] = x[half:]
        for k in range(wide // HD):
            piece = x[:, k * HD : (k + 1) * HD]
            squares = squares + piece * piece
    rstd = lax.rsqrt(jnp.sum(squares, -1, keepdims=True) / d + 1e-06)
    scaled = lat2 * rstd
    scaled_high = scaled.astype(BF16).astype(F32)
    lane = lax.broadcasted_iota(jnp.int32, (rows, 2 * ch), 1)
    scaled = jnp.where(lane < ch, scaled_high, scaled - scaled_high).astype(BF16)
    lall[1 - c, 0] = scaled[0:half]
    lall[c, 0] = scaled[half:]
    lat_out = [
        remote(
            lall.at[:, 0], lall.at[:, 4 - k], ls.at[k - 1], lr.at[k - 1],
            {"mp": lax.rem(m + k, n_mp)},
        )
        for k in (1, 2, 3)
    ]
    for copy in lat_out:
        copy.start()

    c_text[1].wait()
    norm_text(1)
    c_text[3].wait()
    norm_text(3)
    to_right[1].start()
    to_left[3].start()
    to_right[2].start()
    to_left[0].start()
    to_right[3].start()
    to_left[1].start()
    c_wo = local_copy(wo_h, wo, 6 + heads)
    c_wf = local_copy(wf_h, wf, 7 + heads)
    c_mfin = local_copy(mfin_h, mfin, 8 + heads)

    s_high, s_low = split(w * (1.0 + mimg[1, pl.ds(step, 1), :]))
    lhs[0:ch, :] = s_high
    lhs[ch : 2 * ch, :] = s_low
    b_high, b_low = split(mimg[0, pl.ds(step, 1), :])
    b_row = lax.broadcasted_iota(jnp.int32, (16, d), 0)
    lhs[2 * ch :, :] = jnp.where(
        b_row == 0, b_high.astype(F32), jnp.where(b_row == 1, b_low.astype(F32), 0.0)
    ).astype(BF16)

    def fill_mask(ref, img_live, txt_live, on):
        spot = lax.broadcasted_iota(jnp.int32, (half, HD), 0)
        for side in range(2):
            place = (1 - c) if side == 0 else c
            for k in range(4):
                start = lax.rem(m + k, n_mp) * rows + place * half
                at = side * 4 * half + k * half
                ref[at : at + half, :] = jnp.where(spot + start < img_live, on, 0.0).astype(BF16)
        spot_t = lax.broadcasted_iota(jnp.int32, (trows, HD), 0)
        for k in range(4):
            start = lax.rem(m + TEXT_FROM[k], n_mp) * trows
            ref[img + k * trows : img + (k + 1) * trows, :] = jnp.where(
                spot_t + start < txt_live, on, 0.0
            ).astype(BF16)

    fill_mask(mask, il, tl, 1.0)
    fill_mask(maskm, il_m, tl_m, flag)

    for h in range(heads):
        c_wq[h].wait()
        full = dot(lhs[...], wq[h])
        fold = full[0:ch] + full[ch : 2 * ch]
        high, low = split(fold)
        rhs[h, 0:ch, :] = high
        rhs[h, ch : 2 * ch, :] = high
        rhs[h, 2 * ch : 3 * ch, :] = low
        rhs[h, 3 * ch : 4 * ch, :] = low
        bias[h] = full[2 * ch : 2 * ch + 8]
    for copy in lat_out:
        copy.wait_recv()
    q_gain = qg[...] * (HD ** (-0.5) * math.log2(math.e))
    k_gain = kg[...]
    block_rows = 4 * half

    def image_block(side, carry):
        block = jnp.concatenate([lall[side, k] for k in range(4)], axis=0)
        block = jnp.concatenate([block, block], axis=1)
        at = pl.ds(pl.multiple_of(side * block_rows, block_rows), block_rows)
        for h in range(heads):
            x = dot(block, rhs[h]) + (bias[h, 0:1, :] + bias[h, 1:2, :])
            q[h, at, :] = head_norm(x[:, 0:HD], q_gain).astype(BF16)
            kv[h, at, 0:HD] = head_norm(x[:, HD : 2 * HD], k_gain).astype(BF16)
            kv[h, at, HD : 2 * HD] = x[:, 2 * HD :].astype(BF16) * mask[at, :]
        return carry

    lax.fori_loop(0, 2, image_block, 0)
    kv_img = [
        remote(
            kv.at[h, pl.ds(0, img)], kvm.at[h, pl.ds(0, img)], ks.at[h], kr.at[h],
            {"group": mate},
        )
        for h in range(heads)
    ]
    for copy in kv_img:
        copy.start()

    def text_block(first, count):
        span = slice(img + first * trows, img + (first + count) * trows)
        lhs_t = txt[first] if count == 1 else jnp.concatenate(
            [txt[first + k] for k in range(count)], axis=0
        )
        copies = []
        for h in range(heads):
            x = dot(lhs_t, wt[:, h * 2 * HD : (h + 1) * 2 * HD])
            kv[h, span, 0:HD] = head_norm(x[:, 0:HD], k_gain).astype(BF16)
            kv[h, span, HD : 2 * HD] = x[:, HD:].astype(BF16) * mask[span, :]
            i = heads + (first if first < 2 else 2) * heads + h
            rows_t = pl.ds(img + first * trows, count * trows)
            copy = remote(
                kv.at[h, rows_t], kvm.at[h, rows_t], ks.at[i], kr.at[i], {"group": mate}
            )
            copy.start()
            copies.append(copy)
        return copies

    c_wt.wait()
    kv_txt = text_block(0, 1)
    on = flag.astype(BF16)

    def keys(h, parts):
        return jnp.concatenate([ref[h, lo : lo + n, 0:HD] for ref, lo, n in parts], axis=0)

    def values(h, parts):
        rows_v = []
        for ref, lo, n in parts:
            v = ref[h, lo : lo + n, HD : 2 * HD]
            if ref is kvm:
                v = v * on
            live = (maskm if ref is kvm else mask)[lo : lo + n, :]
            rows_v.append(jnp.concatenate([v, live], axis=1))
        return jnp.concatenate(rows_v, axis=0)

    def attend(h, at, parts):
        p = jnp.exp2(nt_dot(q[h, at, :], keys(h, parts))).astype(BF16)
        return dot(p, values(h, parts))

    def each_side(fn):
        def run(side, carry):
            at = pl.ds(pl.multiple_of(side * block_rows, block_rows), block_rows)
            for h in range(heads):
                fn(h, at)
            return carry

        lax.fori_loop(0, 2, run, 0)

    def own_image(h, at):
        acc[h, at, :] = attend(h, at, [(kv, 0, img)])

    each_side(own_image)

    to_right[0].wait_recv()
    on_right[0].start()
    to_left[2].wait_recv()
    on_left[0].start()
    for copy in kv_img:
        copy.wait_recv()

    def mate_image(h, at):
        acc[h, at, :] += attend(h, at, [(kvm, 0, img)])

    each_side(mate_image)

    to_right[1].wait_recv()
    on_right[1].start()
    to_left[3].wait_recv()
    on_left[1].start()
    to_right[2].wait_recv()
    to_right[3].wait_recv()
    to_left[0].wait_recv()
    to_left[1].wait_recv()
    kv_txt += text_block(1, 2)
    for copy in kv_txt:
        copy.wait_recv()

    def most_text(h, at):
        acc[h, at, :] += attend(h, at, [(kv, img, 3 * trows), (kvm, img, 3 * trows)])

    each_side(most_text)

    for copy in on_right + on_left:
        copy.wait_recv()
    kv_last = text_block(3, 1)
    last = img + 3 * trows

    mixes = []
    for side in range(2):
        for h in range(heads):
            if side == 0:
                kv_last[h].wait_recv()
            at = slice(side * block_rows, (side + 1) * block_rows)
            total = acc[h, at, :] + attend(h, at, [(kv, last, trows), (kvm, last, trows)])
            share = (total[:, 0:HD] / total[:, HD : 2 * HD]).astype(BF16)
            for k in range(4):
                mix[side, k, h] = share[k * half : (k + 1) * half]
        copies = {}
        for k in (2, 1, 3):
            i = side * 3 + k - 1
            copies[k] = remote(
                mix.at[side, k], mixr.at[side, 3 - k], ms.at[i], mr.at[i],
                {"mp": lax.rem(m + k, n_mp)},
            )
            copies[k].start()
        mixes.append(copies)

    def project(side, ref, k, first):
        base = pl.multiple_of(lax.rem(m + k, n_mp) * (heads * HD), heads * HD)
        own = jnp.concatenate([ref[h] for h in range(heads)], axis=1)
        for j in range(d // wide):
            cols = slice(j * wide, (j + 1) * wide)
            x = dot(own, wo[pl.ds(base, heads * HD), cols])
            att[side, :, cols] = x if first else att[side, :, cols] + x

    def finish(side):
        small = min(half, 32)
        for i in range(half // small):
            at = slice(i * small, (i + 1) * small)
            x = xc[side, at, :] + mimg[2, pl.ds(step, 1), :] * att[side, at, :]
            center = x - jnp.mean(x, -1, keepdims=True)
            spread = jnp.mean(center * center, -1, keepdims=True)
            y = center * lax.rsqrt(spread + 1e-06) * (1.0 + mfin[step, 1:2, :]) + mfin[step, 0:1, :]
            fin[at, :] = y.astype(BF16)
        return nt_dot(wf[...], fin[...])

    c_wo.wait()
    project(0, mix.at[0, 0], 0, True)
    project(1, mix.at[1, 0], 0, True)
    c_wf.wait()
    c_mfin.wait()
    for k in (2, 1, 3):
        mixes[0][k].wait_recv()
        project(0, mixr.at[0, 3 - k], 4 - k, False)
    vsend[...] = finish(0)
    swap = remote(vsend, vrecv, vs.at[0], vr.at[0], {"cfg": 1 - c})
    swap.start()
    for k in (2, 1, 3):
        mixes[1][k].wait_recv()
        project(1, mixr.at[1, 3 - k], 4 - k, False)
    own = finish(1)
    swap.wait_recv()
    other = vrecv[...]
    cond = jnp.where(c == 0, own, other)
    uncond = jnp.where(c == 0, other, own)
    guided = uncond + guide[g] * (cond - uncond)
    spot = lax.broadcasted_iota(jnp.int32, (ch, half), 1) + (m * rows + c * half)
    guided = jnp.where(spot < il, guided, 0.0)
    vel_o[...] = guided
    next_o[...] = lat[:, pl.ds(pl.multiple_of(c * half, half), half)] - step_size[step] * guided

    for copy in to_right + to_left + on_right + on_left + lat_out + kv_img + kv_txt + kv_last:
        copy.wait_send()
    for copies in mixes:
        for k in (2, 1, 3):
            copies[k].wait_send()
    swap.wait_send()


def local(
    latents, text_hidden, w_img_in, w_img_qkv, w_txt_kv, q_gain, k_gain, w_out, w_final,
    mod_img, mod_txt, mod_final, guide, step_size, img_len, txt_len, split_flag, tstep,
):
    text = text_hidden[0]
    rows, ch = latents.shape
    trows, d = text.shape
    heads = w_img_qkv.shape[1] // (3 * HD)
    img, ntxt = 4 * rows, 4 * trows
    half = rows // 2
    hbm = pl.BlockSpec(memory_space=pl.ANY)
    vmem = pl.BlockSpec(memory_space=pltpu.VMEM)
    smem = pl.BlockSpec(memory_space=pltpu.SMEM)
    dma = pltpu.SemaphoreType.DMA
    out = jax.ShapeDtypeStruct((ch, half), F32)
    scratch = [
        pltpu.VMEM((ch, rows), F32),
        pltpu.VMEM(text.shape, BF16),
        pltpu.VMEM(w_img_in.shape, BF16),
        pltpu.VMEM((heads, d, 3 * HD), BF16),
        pltpu.VMEM(w_txt_kv.shape, BF16),
        pltpu.VMEM(w_out.shape, BF16),
        pltpu.VMEM((ch, d), BF16),
        pltpu.VMEM((3, mod_img.shape[0], d), F32),
        pltpu.VMEM(mod_txt.shape, F32),
        pltpu.VMEM(mod_final.shape, F32),
        pltpu.VMEM((4, trows, d), BF16),
        pltpu.VMEM((2, 4, half, 2 * ch), BF16),
        pltpu.VMEM((2 * ch, d), BF16),
        pltpu.VMEM((2 * ch + 16, d), BF16),
        pltpu.VMEM((heads, 4 * ch, 3 * HD), BF16),
        pltpu.VMEM((heads, 8, 3 * HD), F32),
        pltpu.VMEM((2, half, d), F32),
        pltpu.VMEM((heads, img, HD), BF16),
        pltpu.VMEM((heads, img + ntxt, 2 * HD), BF16),
        pltpu.VMEM((heads, img + ntxt, 2 * HD), BF16),
        pltpu.VMEM((img + ntxt, HD), BF16),
        pltpu.VMEM((img + ntxt, HD), BF16),
        pltpu.VMEM((heads, img, 2 * HD), F32),
        pltpu.VMEM((2, half, d), F32),
        pltpu.VMEM((2, 4, heads, half, HD), BF16),
        pltpu.VMEM((2, 3, heads, half, HD), BF16),
        pltpu.VMEM((half, d), BF16),
        pltpu.VMEM((ch, half), F32),
        pltpu.VMEM((ch, half), F32),
        dma((13 + heads,)),
        dma((12,)), dma((12,)),
        dma((3,)), dma((3,)),
        dma((4 * heads,)), dma((4 * heads,)),
        dma((6,)), dma((6,)),
        dma((1,)), dma((1,)),
    ]
    velocity, moved = pl.pallas_call(
        body,
        out_shape=(out, out),
        in_specs=[hbm] * 10 + [vmem] * 2 + [smem] * 6,
        out_specs=(vmem, vmem),
        scratch_shapes=scratch,
        compiler_params=pltpu.CompilerParams(
            collective_id=0, has_side_effects=True, vmem_limit_bytes=61 * 1024 * 1024
        ),
        name="guided_step",
    )(
        latents.T, text, w_img_in, w_img_qkv, w_txt_kv, w_out, w_final.T,
        jnp.transpose(mod_img, (1, 0, 2)), mod_txt, mod_final,
        q_gain[None], k_gain[None], guide, step_size, img_len, txt_len, split_flag, tstep,
    )
    return velocity.T[None], moved.T[None]


def solution(mesh):
    rep = P()
    placed = (
        P(("group", "mp"), None), P("cfg", ("group", "mp"), None), rep,
        P(None, "mp"), P(None, "mp"),
    ) + (rep,) * 13
    out = P("cfg", ("group", "mp"), None)
    return jax.shard_map(
        local, mesh=mesh, in_specs=placed, out_specs=(out, out), check_vma=False
    )
```

time: 75.2 us -> 58.3 us (0.78)
  Pallas kernels: 65.4 us -> 54.6 us
  local copies, waits for them, and re-layouts: 8.73 us -> 2.75 us
    pallas_call x1, Pallas kernels: 65.4 us -> 54.6 us  [local(): pl.pallas_call(body, out_shape=(out, out), in_specs=[hbm] * 10 + [vmem] *...]
    unnamed x5 -> x2, local copies, waits for them, and re-layouts: 8.73 us -> 2.75 us
where the time goes in v3:
time: 58.3 us; the launch traced here: 58 us
  Pallas kernels  54.6 us (94%)
  local copies, waits for them, and re-layouts  2.75 us (5%)
  between operations  0.65 us (1%)
    pallas_call x1, Pallas kernels, local(): pl.pallas_call(body, out_shape=(out, out), in_specs=[hbm] * 10 + [vmem] *...  54.6 us
    unnamed x2, local copies, waits for them, and re-layouts  2.75 us

profile of v3, /device:TPU:0, one launch (start us, length us, event | category | flops | bytes accessed | tf_op | source)
XLA Modules:
  0.0 58.0 jit_solution(6669982781394876044)
XLA Ops:
  0.6 54.6 %guided_step.1 = (f32[64,128]{1,0:T(8,128)}, f32[64,128]{1,0:T(8,128)}) custom-call(f32[64,256]{1,0:T(8,128)} %bitcast.15, bf16[128,3072]{1,0:T(8,128)(2,1)} %bitcast.12, bf16[64,3072]{1,0:T(8,128)(2,1)} %win_h.1, bf16[3072,1152]{1,0:T(8,128)(2,1)} %wq_h.1, bf16[3072,768]{1,0:T(8,128)(2,1)} %wt_h.1, bf16[1536,3072]{1,0:T(8,128)(2,1)} %wo_h.1, ...), custom_call_target="tpu_custom_call" | custom-call | tf_op jit(solution)/shard_map/guided_step/pallas_call | solution.py:463
  55.3 1.4 %copy.22 = f32[1,128,64]{1,2,0:T(8,128)} copy(f32[1,128,64]{1,2,0:T(8,128)} %bitcast.17) | data formatting | bytes 65536
  56.6 1.4 %copy.23 = f32[1,128,64]{1,2,0:T(8,128)} copy(f32[1,128,64]{1,2,0:T(8,128)} %bitcast.16) | data formatting | bytes 65536

commit v4 on v3

--- a/solution.py
+++ b/solution.py
@@ -35,7 +35,7 @@
 def body(
     lat_h, text_h, win_h, wq_h, wt_h, wo_h, wf_h, mimg_h, mtxt_h, mfin_h,
     qg, kg, guide, step_size, img_len, txt_len, flags, tstep,
-    vel_o, next_o,
+    out,
     lat, text, win, wq, wt, wo, wf, mimg, mtxt, mfin,
     txt, lall, wx, lhs, rhs, bias, xc, q, kv, kvm, mask, maskm, acc, att,
     mix, mixr, fin, vsend, vrecv,
@@ -62,15 +62,11 @@
         copy.start()
         return copy
 
-    c_text = {
-        i: local_copy(text_h.at[chunk(i)], text.at[chunk(i)], 9 + heads + i) for i in (0, 2)
-    }
-    c_mtxt = local_copy(mtxt_h, mtxt, 1)
     c_lat = local_copy(lat_h, lat, 2)
     c_win = local_copy(win_h, win, 3)
+    c_mtxt = local_copy(mtxt_h, mtxt, 1)
+    c_text = local_copy(text_h, text, 0)
     c_mimg = local_copy(mimg_h, mimg, 4)
-    for i in (1, 3):
-        c_text[i] = local_copy(text_h.at[chunk(i)], text.at[chunk(i)], 9 + heads + i)
 
     barrier = pltpu.get_barrier_semaphore()
     for k in (1, 2, 3):
@@ -91,12 +87,15 @@
     il_m, tl_m = img_len[mate], txt_len[mate]
     flag = jnp.where(flags[c, g] == 1, 1.0, 0.0).astype(F32)
 
+    def source(i, first):
+        return text_h.at[chunk(i)] if i == first else txt.at[0, chunk(i)]
+
     to_right = [
-        remote(txt.at[0, chunk(i)], txt.at[2, chunk(i)], ts.at[i], tr.at[i], {"mp": right})
+        remote(source(i, 0), txt.at[2, chunk(i)], ts.at[i], tr.at[i], {"mp": right})
         for i in range(4)
     ]
     to_left = [
-        remote(txt.at[0, chunk(i)], txt.at[1, chunk(i)], ts.at[4 + i], tr.at[4 + i], {"mp": left})
+        remote(source(i, 2), txt.at[1, chunk(i)], ts.at[4 + i], tr.at[4 + i], {"mp": left})
         for i in range(4)
     ]
     on_right = [
@@ -108,28 +107,18 @@
         for i in (2, 3)
     ]
 
-    def norm_text(i):
-        x = text[chunk(i), :].astype(F32)
+    def norm_text(i, slot=0):
+        x = (text[chunk(i), :] if slot == 0 else txt[slot, chunk(i), :]).astype(F32)
         center = x - jnp.mean(x, -1, keepdims=True)
         spread = jnp.mean(center * center, -1, keepdims=True)
         y = center * lax.rsqrt(spread + 1e-06) * (1.0 + mtxt[step, 1:2, :]) + mtxt[step, 0:1, :]
-        txt[0, chunk(i), :] = y.astype(BF16)
-
-    c_mtxt.wait()
-    c_text[0].wait()
-    norm_text(0)
-    c_text[2].wait()
-    norm_text(2)
+        txt[slot, chunk(i), :] = y.astype(BF16)
+
     pl.semaphore_wait(barrier, 5)
     to_right[0].start()
     to_left[2].start()
     c_lat.wait()
     c_win.wait()
-    c_mimg.wait()
-    c_wq = [
-        local_copy(wq_h.at[:, pl.ds(h * 3 * HD, 3 * HD)], wq.at[h], 5 + h) for h in range(heads)
-    ]
-    c_wt = local_copy(wt_h, wt, 5 + heads)
 
     e_row = lax.broadcasted_iota(jnp.int32, (ch, 2 * ch), 0)
     e_col = lax.broadcasted_iota(jnp.int32, (ch, 2 * ch), 1)
@@ -169,13 +158,20 @@
     for copy in lat_out:
         copy.start()
 
-    c_text[1].wait()
+    c_mtxt.wait()
+    c_text.wait()
+    c_mimg.wait()
+    c_wq = [
+        local_copy(wq_h.at[:, pl.ds(h * 3 * HD, 3 * HD)], wq.at[h], 5 + h) for h in range(heads)
+    ]
+    c_wt = local_copy(wt_h, wt, 5 + heads)
     norm_text(1)
-    c_text[3].wait()
+    to_right[1].start()
     norm_text(3)
-    to_right[1].start()
     to_left[3].start()
+    norm_text(2)
     to_right[2].start()
+    norm_text(0)
     to_left[0].start()
     to_right[3].start()
     to_left[1].start()
@@ -303,8 +299,10 @@
     each_side(own_image)
 
     to_right[0].wait_recv()
+    norm_text(0, slot=2)
     on_right[0].start()
     to_left[2].wait_recv()
+    norm_text(2, slot=1)
     on_left[0].start()
     for copy in kv_img:
         copy.wait_recv()
@@ -338,6 +336,7 @@
 
     mixes = []
     for side in range(2):
+        copies = {k: [] for k in (1, 2, 3)}
         for h in range(heads):
             if side == 0:
                 kv_last[h].wait_recv()
@@ -346,14 +345,14 @@
             share = (total[:, 0:HD] / total[:, HD : 2 * HD]).astype(BF16)
             for k in range(4):
                 mix[side, k, h] = share[k * half : (k + 1) * half]
-        copies = {}
-        for k in (2, 1, 3):
-            i = side * 3 + k - 1
-            copies[k] = remote(
-                mix.at[side, k], mixr.at[side, 3 - k], ms.at[i], mr.at[i],
-                {"mp": lax.rem(m + k, n_mp)},
-            )
-            copies[k].start()
+            for k in (2, 1, 3):
+                i = (side * 3 + k - 1) * heads + h
+                copy = remote(
+                    mix.at[side, k, h], mixr.at[side, 3 - k, h], ms.at[i], mr.at[i],
+                    {"mp": lax.rem(m + k, n_mp)},
+                )
+                copy.start()
+                copies[k].append(copy)
         mixes.append(copies)
 
     def project(side, ref, k, first):
@@ -380,14 +379,16 @@
     project(1, mix.at[1, 0], 0, True)
     c_wf.wait()
     c_mfin.wait()
-    for k in (2, 1, 3):
-        mixes[0][k].wait_recv()
+    for k in (1, 3, 2):
+        for copy in mixes[0][k]:
+            copy.wait_recv()
         project(0, mixr.at[0, 3 - k], 4 - k, False)
     vsend[...] = finish(0)
     swap = remote(vsend, vrecv, vs.at[0], vr.at[0], {"cfg": 1 - c})
     swap.start()
-    for k in (2, 1, 3):
-        mixes[1][k].wait_recv()
+    for k in (1, 3, 2):
+        for copy in mixes[1][k]:
+            copy.wait_recv()
         project(1, mixr.at[1, 3 - k], 4 - k, False)
     own = finish(1)
     swap.wait_recv()
@@ -397,15 +398,26 @@
     guided = uncond + guide[g] * (cond - uncond)
     spot = lax.broadcasted_iota(jnp.int32, (ch, half), 1) + (m * rows + c * half)
     guided = jnp.where(spot < il, guided, 0.0)
-    vel_o[...] = guided
-    next_o[...] = lat[:, pl.ds(pl.multiple_of(c * half, half), half)] - step_size[step] * guided
+    out[0] = guided
+    out[1] = lat[:, pl.ds(pl.multiple_of(c * half, half), half)] - step_size[step] * guided
 
     for copy in to_right + to_left + on_right + on_left + lat_out + kv_img + kv_txt + kv_last:
         copy.wait_send()
     for copies in mixes:
         for k in (2, 1, 3):
-            copies[k].wait_send()
+            for copy in copies[k]:
+                copy.wait_send()
     swap.wait_send()
+
+
+def unpack(both, velocity, moved, sem):
+    copies = [
+        pltpu.make_async_copy(both.at[i], ref, sem.at[i]) for i, ref in enumerate((velocity, moved))
+    ]
+    for copy in copies:
+        copy.start()
+    for copy in copies:
+        copy.wait()
 
 
 def local(
@@ -422,7 +434,8 @@
     vmem = pl.BlockSpec(memory_space=pltpu.VMEM)
     smem = pl.BlockSpec(memory_space=pltpu.SMEM)
     dma = pltpu.SemaphoreType.DMA
-    out = jax.ShapeDtypeStruct((ch, half), F32)
+    out = jax.ShapeDtypeStruct((2, ch, half), F32)
+    single = jax.ShapeDtypeStruct((ch, half), F32)
     scratch = [
         pltpu.VMEM((ch, rows), F32),
         pltpu.VMEM(text.shape, BF16),
@@ -457,14 +470,14 @@
         dma((12,)), dma((12,)),
         dma((3,)), dma((3,)),
         dma((4 * heads,)), dma((4 * heads,)),
-        dma((6,)), dma((6,)),
+        dma((6 * heads,)), dma((6 * heads,)),
         dma((1,)), dma((1,)),
     ]
-    velocity, moved = pl.pallas_call(
+    both = pl.pallas_call(
         body,
-        out_shape=(out, out),
+        out_shape=out,
         in_specs=[hbm] * 10 + [vmem] * 2 + [smem] * 6,
-        out_specs=(vmem, vmem),
+        out_specs=vmem,
         scratch_shapes=scratch,
         compiler_params=pltpu.CompilerParams(
             collective_id=0, has_side_effects=True, vmem_limit_bytes=61 * 1024 * 1024
@@ -475,6 +488,14 @@
         jnp.transpose(mod_img, (1, 0, 2)), mod_txt, mod_final,
         q_gain[None], k_gain[None], guide, step_size, img_len, txt_len, split_flag, tstep,
     )
+    velocity, moved = pl.pallas_call(
+        unpack,
+        out_shape=(single, single),
+        in_specs=[hbm],
+        out_specs=(hbm, hbm),
+        scratch_shapes=[dma((2,))],
+        name="unpack",
+    )(both)
     return velocity.T[None], moved.T[None]
 
 

time: 58.3 us -> 58.4 us (level)
  Pallas kernels: 54.6 us -> 57.5 us
  local copies, waits for them, and re-layouts: 2.75 us -> 0 us
    pallas_call x1 -> x2, Pallas kernels: 54.6 us -> 57.5 us  [the longest x1 54.3 us: local(): pl.pallas_call(body, out_shape=out, in_specs=[hbm] * 10 + [vmem] * 2 + [s...]
    unnamed x2 -> x0, local copies, waits for them, and re-layouts: 2.75 us -> none
where the time goes in v4:
time: 58.4 us; the launch traced here: 58.3 us
  Pallas kernels  57.5 us (98%)
  between operations  0.83 us (1%)
    pallas_call x1, Pallas kernels, local(): pl.pallas_call(body, out_shape=out, in_specs=[hbm] * 10 + [vmem] * 2 + [s...  54.3 us
    pallas_call x1, Pallas kernels, local(): pl.pallas_call(unpack, out_shape=(single, single), in_specs=[hbm], out_sp...  3.11 us

profile of v4, /device:TPU:0, one launch (start us, length us, event | category | flops | bytes accessed | tf_op | source)
XLA Modules:
  0.0 58.3 jit_solution(3053097537135130221)
XLA Ops:
  0.6 54.3 %guided_step.1.both = f32[2,64,128]{2,1,0:T(8,128)} custom-call(f32[64,256]{1,0:T(8,128)} %bitcast.15, bf16[128,3072]{1,0:T(8,128)(2,1)} %bitcast.12, bf16[64,3072]{1,0:T(8,128)(2,1)} %win_h.1, bf16[3072,1152]{1,0:T(8,128)(2,1)} %wq_h.1, bf16[3072,768]{1,0:T(8,128)(2,1)} %wt_h.1, bf16[1536,3072]{1,0:T(8,128)(2,1)} %wo_h.1, bf16[64,3072]{1,0:T(8,128)(2,1)} %bitcast.13, ...), custom_call_target="tpu_custom_call" | custom-call | tf_op jit(solution)/shard_map/guided_step/pallas_call | solution.py:476
  55.0 3.1 %unpack.1 = (f32[64,128]{1,0:T(8,128)}, f32[64,128]{1,0:T(8,128)}) custom-call(f32[2,64,128]{2,1,0:T(8,128)} %guided_step.1.both), custom_call_target="tpu_custom_call" | custom-call | tf_op jit(solution)/shard_map/unpack/pallas_call | solution.py:491

commit v5 on v4

--- a/solution.py
+++ b/solution.py
@@ -117,40 +117,21 @@
     pl.semaphore_wait(barrier, 5)
     to_right[0].start()
     to_left[2].start()
-    c_lat.wait()
-    c_win.wait()
-
+
+    quarter = half // 2
     e_row = lax.broadcasted_iota(jnp.int32, (ch, 2 * ch), 0)
     e_col = lax.broadcasted_iota(jnp.int32, (ch, 2 * ch), 1)
     twice = jnp.where((e_col == e_row) | (e_col == e_row + ch), 1.0, 0.0).astype(BF16)
-    lat2 = lax.dot_general(
-        lat[...].astype(BF16), twice, (((0,), (0,)), ((), ())), preferred_element_type=F32
+    c_lat.wait()
+    lines = lax.dot_general(
+        lat[:, pl.ds(pl.multiple_of((1 - c) * half, half), half)].astype(BF16), twice,
+        (((0,), (0,)), ((), ())), preferred_element_type=F32,
     )
-    w = win[...].astype(F32)
-    w = w - jnp.mean(w, -1, keepdims=True)
-    w_high, w_low = split(w)
-    wx[0:ch, :] = w_high
-    wx[ch : 2 * ch, :] = w_low
-    lat2b = lat2.astype(BF16)
-    squares = jnp.zeros((rows, HD), F32)
-    wide = min(d, 512)
-    for j in range(d // wide):
-        x = dot(lat2b, wx[:, j * wide : (j + 1) * wide])
-        xc[1 - c, :, j * wide : (j + 1) * wide] = x[0:half]
-        xc[c, :, j * wide : (j + 1) * wide] = x[half:]
-        for k in range(wide // HD):
-            piece = x[:, k * HD : (k + 1) * HD]
-            squares = squares + piece * piece
-    rstd = lax.rsqrt(jnp.sum(squares, -1, keepdims=True) / d + 1e-06)
-    scaled = lat2 * rstd
-    scaled_high = scaled.astype(BF16).astype(F32)
-    lane = lax.broadcasted_iota(jnp.int32, (rows, 2 * ch), 1)
-    scaled = jnp.where(lane < ch, scaled_high, scaled - scaled_high).astype(BF16)
-    lall[1 - c, 0] = scaled[0:half]
-    lall[c, 0] = scaled[half:]
+    lane = lax.broadcasted_iota(jnp.int32, (quarter, 2 * ch), 1)
+    lall[0, 0] = jnp.where(lane < ch, lines[0:quarter], lines[quarter:]).astype(BF16)
     lat_out = [
         remote(
-            lall.at[:, 0], lall.at[:, 4 - k], ls.at[k - 1], lr.at[k - 1],
+            lall.at[0, 0], lall.at[0, 4 - k], ls.at[k - 1], lr.at[k - 1],
             {"mp": lax.rem(m + k, n_mp)},
         )
         for k in (1, 2, 3)
@@ -179,6 +160,12 @@
     c_wf = local_copy(wf_h, wf, 7 + heads)
     c_mfin = local_copy(mfin_h, mfin, 8 + heads)
 
+    c_win.wait()
+    w = win[...].astype(F32)
+    w = w - jnp.mean(w, -1, keepdims=True)
+    w_high, w_low = split(w)
+    wx[0:ch, :] = w_high
+    wx[ch : 2 * ch, :] = w_low
     s_high, s_low = split(w * (1.0 + mimg[1, pl.ds(step, 1), :]))
     lhs[0:ch, :] = s_high
     lhs[ch : 2 * ch, :] = s_low
@@ -199,8 +186,11 @@
         spot_t = lax.broadcasted_iota(jnp.int32, (trows, HD), 0)
         for k in range(4):
             start = lax.rem(m + TEXT_FROM[k], n_mp) * trows
+            place = jnp.where((spot_t >= part) & (spot_t < 2 * part), spot_t + part, jnp.where(
+                (spot_t >= 2 * part) & (spot_t < 3 * part), spot_t - part, spot_t
+            )) if k == 3 else spot_t
             ref[img + k * trows : img + (k + 1) * trows, :] = jnp.where(
-                spot_t + start < txt_live, on, 0.0
+                place + start < txt_live, on, 0.0
             ).astype(BF16)
 
     fill_mask(mask, il, tl, 1.0)
@@ -218,12 +208,56 @@
         bias[h] = full[2 * ch : 2 * ch + 8]
     for copy in lat_out:
         copy.wait_recv()
+    lat_swap = remote(lall.at[0], lall.at[1], ls.at[3], lr.at[3], {"cfg": 1 - c})
+    lat_swap.start()
     q_gain = qg[...] * (HD ** (-0.5) * math.log2(math.e))
     k_gain = kg[...]
     block_rows = 4 * half
 
+    def text_block(lhs_t, first, i):
+        n = lhs_t.shape[0]
+        span = slice(img + first, img + first + n)
+        copies = []
+        for h in range(heads):
+            x = dot(lhs_t, wt[:, h * 2 * HD : (h + 1) * 2 * HD])
+            kv[h, span, 0:HD] = head_norm(x[:, 0:HD], k_gain).astype(BF16)
+            kv[h, span, HD : 2 * HD] = x[:, HD:].astype(BF16) * mask[span, :]
+            rows_t = pl.ds(img + first, n)
+            copy = remote(
+                kv.at[h, rows_t], kvm.at[h, rows_t], ks.at[i * heads + h], kr.at[i * heads + h],
+                {"group": mate},
+            )
+            copy.start()
+            copies.append(copy)
+        return copies
+
+    c_wt.wait()
+    kv_txt = text_block(txt[0], 0, 1)
+    lat_swap.wait_recv()
+    wide = min(d, 512)
+
     def image_block(side, carry):
-        block = jnp.concatenate([lall[side, k] for k in range(4)], axis=0)
+        held = jnp.concatenate([lall[side, k] for k in range(4)], axis=0)
+        pick = lax.broadcasted_iota(jnp.int32, (2 * ch, 2 * ch), 0)
+        lane_of = lax.rem(lax.broadcasted_iota(jnp.int32, (2 * ch, 2 * ch), 1), ch)
+        top = dot(held, jnp.where(pick == lane_of, 1.0, 0.0).astype(BF16))
+        low = dot(held, jnp.where(pick == lane_of + ch, 1.0, 0.0).astype(BF16))
+        pieces = []
+        for k in range(4):
+            pieces += [top[k * quarter : (k + 1) * quarter], low[k * quarter : (k + 1) * quarter]]
+        lat2 = jnp.concatenate(pieces, axis=0)
+        lat2b = lat2.astype(BF16)
+        squares = jnp.zeros((block_rows, HD), F32)
+        for j in range(d // wide):
+            x = dot(lat2b, wx[:, j * wide : (j + 1) * wide])
+            xc[side, :, j * wide : (j + 1) * wide] = x[0:half]
+            for k in range(wide // HD):
+                piece = x[:, k * HD : (k + 1) * HD]
+                squares = squares + piece * piece
+        scaled = lat2 * lax.rsqrt(jnp.sum(squares, -1, keepdims=True) / d + 1e-06)
+        scaled_high = scaled.astype(BF16).astype(F32)
+        lanes = lax.broadcasted_iota(jnp.int32, (block_rows, 2 * ch), 1)
+        block = jnp.where(lanes < ch, scaled_high, scaled - scaled_high).astype(BF16)
         block = jnp.concatenate([block, block], axis=1)
         at = pl.ds(pl.multiple_of(side * block_rows, block_rows), block_rows)
         for h in range(heads):
@@ -244,27 +278,6 @@
     for copy in kv_img:
         copy.start()
 
-    def text_block(first, count):
-        span = slice(img + first * trows, img + (first + count) * trows)
-        lhs_t = txt[first] if count == 1 else jnp.concatenate(
-            [txt[first + k] for k in range(count)], axis=0
-        )
-        copies = []
-        for h in range(heads):
-            x = dot(lhs_t, wt[:, h * 2 * HD : (h + 1) * 2 * HD])
-            kv[h, span, 0:HD] = head_norm(x[:, 0:HD], k_gain).astype(BF16)
-            kv[h, span, HD : 2 * HD] = x[:, HD:].astype(BF16) * mask[span, :]
-            i = heads + (first if first < 2 else 2) * heads + h
-            rows_t = pl.ds(img + first * trows, count * trows)
-            copy = remote(
-                kv.at[h, rows_t], kvm.at[h, rows_t], ks.at[i], kr.at[i], {"group": mate}
-            )
-            copy.start()
-            copies.append(copy)
-        return copies
-
-    c_wt.wait()
-    kv_txt = text_block(0, 1)
     on = flag.astype(BF16)
 
     def keys(h, parts):
@@ -320,7 +333,7 @@
     to_right[3].wait_recv()
     to_left[0].wait_recv()
     to_left[1].wait_recv()
-    kv_txt += text_block(1, 2)
+    kv_txt += text_block(jnp.concatenate([txt[1], txt[2]], axis=0), trows, 2)
     for copy in kv_txt:
         copy.wait_recv()
 
@@ -329,9 +342,12 @@
 
     each_side(most_text)
 
-    for copy in on_right + on_left:
-        copy.wait_recv()
-    kv_last = text_block(3, 1)
+    kv_last = []
+    for i in range(2):
+        on_right[i].wait_recv()
+        on_left[i].wait_recv()
+        lhs_t = jnp.concatenate([txt[3, chunk(i), :], txt[3, chunk(2 + i), :]], axis=0)
+        kv_last.append(text_block(lhs_t, 3 * trows + 2 * i * part, 3 + i))
     last = img + 3 * trows
 
     mixes = []
@@ -339,7 +355,8 @@
         copies = {k: [] for k in (1, 2, 3)}
         for h in range(heads):
             if side == 0:
-                kv_last[h].wait_recv()
+                kv_last[0][h].wait_recv()
+                kv_last[1][h].wait_recv()
             at = slice(side * block_rows, (side + 1) * block_rows)
             total = acc[h, at, :] + attend(h, at, [(kv, last, trows), (kvm, last, trows)])
             share = (total[:, 0:HD] / total[:, HD : 2 * HD]).astype(BF16)
@@ -360,14 +377,14 @@
         own = jnp.concatenate([ref[h] for h in range(heads)], axis=1)
         for j in range(d // wide):
             cols = slice(j * wide, (j + 1) * wide)
-            x = dot(own, wo[pl.ds(base, heads * HD), cols])
-            att[side, :, cols] = x if first else att[side, :, cols] + x
+            x = mimg[2, pl.ds(step, 1), cols] * dot(own, wo[pl.ds(base, heads * HD), cols])
+            att[side, :, cols] = (xc if first else att)[side, :, cols] + x
 
     def finish(side):
         small = min(half, 32)
         for i in range(half // small):
             at = slice(i * small, (i + 1) * small)
-            x = xc[side, at, :] + mimg[2, pl.ds(step, 1), :] * att[side, at, :]
+            x = att[side, at, :]
             center = x - jnp.mean(x, -1, keepdims=True)
             spread = jnp.mean(center * center, -1, keepdims=True)
             y = center * lax.rsqrt(spread + 1e-06) * (1.0 + mfin[step, 1:2, :]) + mfin[step, 0:1, :]
@@ -401,23 +418,19 @@
     out[0] = guided
     out[1] = lat[:, pl.ds(pl.multiple_of(c * half, half), half)] - step_size[step] * guided
 
-    for copy in to_right + to_left + on_right + on_left + lat_out + kv_img + kv_txt + kv_last:
+    for copy in to_right + to_left + on_right + on_left + lat_out + kv_img + kv_txt + kv_last[0] + kv_last[1]:
         copy.wait_send()
     for copies in mixes:
         for k in (2, 1, 3):
             for copy in copies[k]:
                 copy.wait_send()
     swap.wait_send()
-
-
-def unpack(both, velocity, moved, sem):
-    copies = [
-        pltpu.make_async_copy(both.at[i], ref, sem.at[i]) for i, ref in enumerate((velocity, moved))
-    ]
-    for copy in copies:
-        copy.start()
-    for copy in copies:
-        copy.wait()
+    lat_swap.wait_send()
+
+
+def unpack(both, velocity, moved):
+    velocity[...] = both[0]
+    moved[...] = both[1]
 
 
 def local(
@@ -448,7 +461,7 @@
         pltpu.VMEM(mod_txt.shape, F32),
         pltpu.VMEM(mod_final.shape, F32),
         pltpu.VMEM((4, trows, d), BF16),
-        pltpu.VMEM((2, 4, half, 2 * ch), BF16),
+        pltpu.VMEM((2, 4, half // 2, 2 * ch), BF16),
         pltpu.VMEM((2 * ch, d), BF16),
         pltpu.VMEM((2 * ch + 16, d), BF16),
         pltpu.VMEM((heads, 4 * ch, 3 * HD), BF16),
@@ -468,8 +481,8 @@
         pltpu.VMEM((ch, half), F32),
         dma((13 + heads,)),
         dma((12,)), dma((12,)),
-        dma((3,)), dma((3,)),
-        dma((4 * heads,)), dma((4 * heads,)),
+        dma((4,)), dma((4,)),
+        dma((5 * heads,)), dma((5 * heads,)),
         dma((6 * heads,)), dma((6 * heads,)),
         dma((1,)), dma((1,)),
     ]
@@ -491,9 +504,8 @@
     velocity, moved = pl.pallas_call(
         unpack,
         out_shape=(single, single),
-        in_specs=[hbm],
-        out_specs=(hbm, hbm),
-        scratch_shapes=[dma((2,))],
+        in_specs=[vmem],
+        out_specs=(vmem, vmem),
         name="unpack",
     )(both)
     return velocity.T[None], moved.T[None]

time: 58.4 us -> 61.1 us (1.046); the launches traced: 58.3 us -> 59.9 us
  Pallas kernels: 57.5 us -> 59.3 us
    pallas_call x1, Pallas kernels: 54.3 us -> 57.8 us  [local(): pl.pallas_call(body, out_shape=out, in_specs=[hbm] * 10 + [vmem] * 2 + [s...]
    pallas_call x1, Pallas kernels: 3.11 us -> 1.47 us  [local(): pl.pallas_call(unpack, out_shape=(single, single), in_specs=[vmem], out_s...]
where the time goes in v5:
time: 61.1 us; the launch traced here: 59.9 us
  Pallas kernels  59.3 us (97%)
  between operations  0.65 us (1%)
    pallas_call x1, Pallas kernels, local(): pl.pallas_call(body, out_shape=out, in_specs=[hbm] * 10 + [vmem] * 2 + [s...  57.8 us
    pallas_call x1, Pallas kernels, local(): pl.pallas_call(unpack, out_shape=(single, single), in_specs=[vmem], out_s...  1.47 us

profile of v5, /device:TPU:0, one launch (start us, length us, event | category | flops | bytes accessed | tf_op | source)
XLA Modules:
  0.0 59.9 jit_solution(3249860749261579144)
XLA Ops:
  0.6 57.8 %guided_step.1.both = f32[2,64,128]{2,1,0:T(8,128)} custom-call(f32[64,256]{1,0:T(8,128)} %bitcast.15, bf16[128,3072]{1,0:T(8,128)(2,1)} %bitcast.12, bf16[64,3072]{1,0:T(8,128)(2,1)} %win_h.1, bf16[3072,1152]{1,0:T(8,128)(2,1)} %wq_h.1, bf16[3072,768]{1,0:T(8,128)(2,1)} %wt_h.1, bf16[1536,3072]{1,0:T(8,128)(2,1)} %wo_h.1, bf16[64,3072]{1,0:T(8,128)(2,1)} %bitcast.13, ...), custom_call_target="tpu_custom_call" | custom-call | tf_op jit(solution)/shard_map/guided_step/pallas_call | solution.py:489
  58.5 1.5 %unpack.1 = (f32[64,128]{1,0:T(8,128)}, f32[64,128]{1,0:T(8,128)}) custom-call(f32[2,64,128]{2,1,0:T(8,128)} %guided_step.1.both), custom_call_target="tpu_custom_call" | custom-call | tf_op jit(solution)/shard_map/unpack/pallas_call | solution.py:504

commit v6 on v5

--- a/solution.py
+++ b/solution.py
@@ -67,6 +67,10 @@
     c_mtxt = local_copy(mtxt_h, mtxt, 1)
     c_text = local_copy(text_h, text, 0)
     c_mimg = local_copy(mimg_h, mimg, 4)
+    c_wq = [
+        local_copy(wq_h.at[:, pl.ds(h * 3 * HD, 3 * HD)], wq.at[h], 5 + h) for h in range(heads)
+    ]
+    c_wt = local_copy(wt_h, wt, 5 + heads)
 
     barrier = pltpu.get_barrier_semaphore()
     for k in (1, 2, 3):
@@ -142,10 +146,6 @@
     c_mtxt.wait()
     c_text.wait()
     c_mimg.wait()
-    c_wq = [
-        local_copy(wq_h.at[:, pl.ds(h * 3 * HD, 3 * HD)], wq.at[h], 5 + h) for h in range(heads)
-    ]
-    c_wt = local_copy(wt_h, wt, 5 + heads)
     norm_text(1)
     to_right[1].start()
     norm_text(3)
@@ -156,9 +156,6 @@
     to_left[0].start()
     to_right[3].start()
     to_left[1].start()
-    c_wo = local_copy(wo_h, wo, 6 + heads)
-    c_wf = local_copy(wf_h, wf, 7 + heads)
-    c_mfin = local_copy(mfin_h, mfin, 8 + heads)
 
     c_win.wait()
     w = win[...].astype(F32)
@@ -186,11 +183,8 @@
         spot_t = lax.broadcasted_iota(jnp.int32, (trows, HD), 0)
         for k in range(4):
             start = lax.rem(m + TEXT_FROM[k], n_mp) * trows
-            place = jnp.where((spot_t >= part) & (spot_t < 2 * part), spot_t + part, jnp.where(
-                (spot_t >= 2 * part) & (spot_t < 3 * part), spot_t - part, spot_t
-            )) if k == 3 else spot_t
             ref[img + k * trows : img + (k + 1) * trows, :] = jnp.where(
-                place + start < txt_live, on, 0.0
+                spot_t + start < txt_live, on, 0.0
             ).astype(BF16)
 
     fill_mask(mask, il, tl, 1.0)
@@ -232,7 +226,16 @@
         return copies
 
     c_wt.wait()
+    c_wo = local_copy(wo_h, wo, 6 + heads)
+    c_wf = local_copy(wf_h, wf, 7 + heads)
+    c_mfin = local_copy(mfin_h, mfin, 8 + heads)
     kv_txt = text_block(txt[0], 0, 1)
+    to_right[0].wait_recv()
+    norm_text(0, slot=2)
+    on_right[0].start()
+    to_left[2].wait_recv()
+    norm_text(2, slot=1)
+    on_left[0].start()
     lat_swap.wait_recv()
     wide = min(d, 512)
 
@@ -311,12 +314,6 @@
 
     each_side(own_image)
 
-    to_right[0].wait_recv()
-    norm_text(0, slot=2)
-    on_right[0].start()
-    to_left[2].wait_recv()
-    norm_text(2, slot=1)
-    on_left[0].start()
     for copy in kv_img:
         copy.wait_recv()
 
@@ -342,12 +339,9 @@
 
     each_side(most_text)
 
-    kv_last = []
-    for i in range(2):
-        on_right[i].wait_recv()
-        on_left[i].wait_recv()
-        lhs_t = jnp.concatenate([txt[3, chunk(i), :], txt[3, chunk(2 + i), :]], axis=0)
-        kv_last.append(text_block(lhs_t, 3 * trows + 2 * i * part, 3 + i))
+    for copy in on_right + on_left:
+        copy.wait_recv()
+    kv_last = text_block(txt[3], 3 * trows, 3)
     last = img + 3 * trows
 
     mixes = []
@@ -355,8 +349,7 @@
         copies = {k: [] for k in (1, 2, 3)}
         for h in range(heads):
             if side == 0:
-                kv_last[0][h].wait_recv()
-                kv_last[1][h].wait_recv()
+                kv_last[h].wait_recv()
             at = slice(side * block_rows, (side + 1) * block_rows)
             total = acc[h, at, :] + attend(h, at, [(kv, last, trows), (kvm, last, trows)])
             share = (total[:, 0:HD] / total[:, HD : 2 * HD]).astype(BF16)
@@ -377,14 +370,14 @@
         own = jnp.concatenate([ref[h] for h in range(heads)], axis=1)
         for j in range(d // wide):
             cols = slice(j * wide, (j + 1) * wide)
-            x = mimg[2, pl.ds(step, 1), cols] * dot(own, wo[pl.ds(base, heads * HD), cols])
-            att[side, :, cols] = (xc if first else att)[side, :, cols] + x
+            x = dot(own, wo[pl.ds(base, heads * HD), cols])
+            att[side, :, cols] = x if first else att[side, :, cols] + x
 
     def finish(side):
         small = min(half, 32)
         for i in range(half // small):
             at = slice(i * small, (i + 1) * small)
-            x = att[side, at, :]
+            x = xc[side, at, :] + mimg[2, pl.ds(step, 1), :] * att[side, at, :]
             center = x - jnp.mean(x, -1, keepdims=True)
             spread = jnp.mean(center * center, -1, keepdims=True)
             y = center * lax.rsqrt(spread + 1e-06) * (1.0 + mfin[step, 1:2, :]) + mfin[step, 0:1, :]
@@ -396,14 +389,14 @@
     project(1, mix.at[1, 0], 0, True)
     c_wf.wait()
     c_mfin.wait()
-    for k in (1, 3, 2):
+    for k in (2, 1, 3):
         for copy in mixes[0][k]:
             copy.wait_recv()
         project(0, mixr.at[0, 3 - k], 4 - k, False)
     vsend[...] = finish(0)
     swap = remote(vsend, vrecv, vs.at[0], vr.at[0], {"cfg": 1 - c})
     swap.start()
-    for k in (1, 3, 2):
+    for k in (2, 1, 3):
         for copy in mixes[1][k]:
             copy.wait_recv()
         project(1, mixr.at[1, 3 - k], 4 - k, False)
@@ -418,7 +411,7 @@
     out[0] = guided
     out[1] = lat[:, pl.ds(pl.multiple_of(c * half, half), half)] - step_size[step] * guided
 
-    for copy in to_right + to_left + on_right + on_left + lat_out + kv_img + kv_txt + kv_last[0] + kv_last[1]:
+    for copy in to_right + to_left + on_right + on_left + lat_out + kv_img + kv_txt + kv_last:
         copy.wait_send()
     for copies in mixes:
         for k in (2, 1, 3):
@@ -482,7 +475,7 @@
         dma((13 + heads,)),
         dma((12,)), dma((12,)),
         dma((4,)), dma((4,)),
-        dma((5 * heads,)), dma((5 * heads,)),
+        dma((4 * heads,)), dma((4 * heads,)),
         dma((6 * heads,)), dma((6 * heads,)),
         dma((1,)), dma((1,)),
     ]

time: 61.1 us -> 57.5 us (0.941)
  Pallas kernels: 59.3 us -> 56 us
    pallas_call x1, Pallas kernels: 57.8 us -> 54.5 us  [local(): pl.pallas_call(body, out_shape=out, in_specs=[hbm] * 10 + [vmem] * 2 + [s...]
where the time goes in v6:
time: 57.5 us; the launch traced here: 56.6 us
  Pallas kernels  56 us (97%)
  between operations  0.65 us (1%)
    pallas_call x1, Pallas kernels, local(): pl.pallas_call(body, out_shape=out, in_specs=[hbm] * 10 + [vmem] * 2 + [s...  54.5 us
    pallas_call x1, Pallas kernels, local(): pl.pallas_call(unpack, out_shape=(single, single), in_specs=[vmem], out_s...  1.47 us

profile of v6, /device:TPU:0, one launch (start us, length us, event | category | flops | bytes accessed | tf_op | source)
XLA Modules:
  0.0 56.6 jit_solution(1825330365850377325)
XLA Ops:
  0.6 54.5 %guided_step.1.both = f32[2,64,128]{2,1,0:T(8,128)} custom-call(f32[64,256]{1,0:T(8,128)} %bitcast.15, bf16[128,3072]{1,0:T(8,128)(2,1)} %bitcast.12, bf16[64,3072]{1,0:T(8,128)(2,1)} %win_h.1, bf16[3072,1152]{1,0:T(8,128)(2,1)} %wq_h.1, bf16[3072,768]{1,0:T(8,128)(2,1)} %wt_h.1, bf16[1536,3072]{1,0:T(8,128)(2,1)} %wo_h.1, bf16[64,3072]{1,0:T(8,128)(2,1)} %bitcast.13, ...), custom_call_target="tpu_custom_call" | custom-call | tf_op jit(solution)/shard_map/guided_step/pallas_call | solution.py:482
  55.1 1.5 %unpack.1 = (f32[64,128]{1,0:T(8,128)}, f32[64,128]{1,0:T(8,128)}) custom-call(f32[2,64,128]{2,1,0:T(8,128)} %guided_step.1.both), custom_call_target="tpu_custom_call" | custom-call | tf_op jit(solution)/shard_map/unpack/pallas_call | solution.py:497

commit v7 on v4

--- a/solution.py
+++ b/solution.py
@@ -379,14 +379,14 @@
     project(1, mix.at[1, 0], 0, True)
     c_wf.wait()
     c_mfin.wait()
-    for k in (1, 3, 2):
+    for k in (2, 1, 3):
         for copy in mixes[0][k]:
             copy.wait_recv()
         project(0, mixr.at[0, 3 - k], 4 - k, False)
     vsend[...] = finish(0)
     swap = remote(vsend, vrecv, vs.at[0], vr.at[0], {"cfg": 1 - c})
     swap.start()
-    for k in (1, 3, 2):
+    for k in (2, 1, 3):
         for copy in mixes[1][k]:
             copy.wait_recv()
         project(1, mixr.at[1, 3 - k], 4 - k, False)
@@ -410,14 +410,9 @@
     swap.wait_send()
 
 
-def unpack(both, velocity, moved, sem):
-    copies = [
-        pltpu.make_async_copy(both.at[i], ref, sem.at[i]) for i, ref in enumerate((velocity, moved))
-    ]
-    for copy in copies:
-        copy.start()
-    for copy in copies:
-        copy.wait()
+def unpack(both, velocity, moved):
+    velocity[...] = both[0]
+    moved[...] = both[1]
 
 
 def local(
@@ -491,9 +486,8 @@
     velocity, moved = pl.pallas_call(
         unpack,
         out_shape=(single, single),
-        in_specs=[hbm],
-        out_specs=(hbm, hbm),
-        scratch_shapes=[dma((2,))],
+        in_specs=[vmem],
+        out_specs=(vmem, vmem),
         name="unpack",
     )(both)
     return velocity.T[None], moved.T[None]

time: 58.4 us -> 56.2 us (0.962)
  Pallas kernels: 57.5 us -> 55.4 us
    pallas_call x1, Pallas kernels: 3.11 us -> 1.47 us  [local(): pl.pallas_call(unpack, out_shape=(single, single), in_specs=[vmem], out_s...]
where the time goes in v7:
time: 56.2 us; the launch traced here: 56 us
  Pallas kernels  55.4 us (99%)
  between operations  0.65 us (1%)
    pallas_call x1, Pallas kernels, local(): pl.pallas_call(body, out_shape=out, in_specs=[hbm] * 10 + [vmem] * 2 + [s...  53.9 us
    pallas_call x1, Pallas kernels, local(): pl.pallas_call(unpack, out_shape=(single, single), in_specs=[vmem], out_s...  1.47 us

profile of v7, /device:TPU:0, one launch (start us, length us, event | category | flops | bytes accessed | tf_op | source)
XLA Modules:
  0.0 56.0 jit_solution(17569642835450719337)
XLA Ops:
  0.6 53.9 %guided_step.1.both = f32[2,64,128]{2,1,0:T(8,128)} custom-call(f32[64,256]{1,0:T(8,128)} %bitcast.15, bf16[128,3072]{1,0:T(8,128)(2,1)} %bitcast.12, bf16[64,3072]{1,0:T(8,128)(2,1)} %win_h.1, bf16[3072,1152]{1,0:T(8,128)(2,1)} %wq_h.1, bf16[3072,768]{1,0:T(8,128)(2,1)} %wt_h.1, bf16[1536,3072]{1,0:T(8,128)(2,1)} %wo_h.1, bf16[64,3072]{1,0:T(8,128)(2,1)} %bitcast.13, ...), custom_call_target="tpu_custom_call" | custom-call | tf_op jit(solution)/shard_map/guided_step/pallas_call | solution.py:471
  54.5 1.5 %unpack.1 = (f32[64,128]{1,0:T(8,128)}, f32[64,128]{1,0:T(8,128)}) custom-call(f32[2,64,128]{2,1,0:T(8,128)} %guided_step.1.both), custom_call_target="tpu_custom_call" | custom-call | tf_op jit(solution)/shard_map/unpack/pallas_call | solution.py:486

commit v8 on v7

--- a/solution.py
+++ b/solution.py
@@ -265,6 +265,12 @@
 
     c_wt.wait()
     kv_txt = text_block(0, 1)
+    to_right[0].wait_recv()
+    norm_text(0, slot=2)
+    on_right[0].start()
+    to_left[2].wait_recv()
+    norm_text(2, slot=1)
+    on_left[0].start()
     on = flag.astype(BF16)
 
     def keys(h, parts):
@@ -298,12 +304,6 @@
 
     each_side(own_image)
 
-    to_right[0].wait_recv()
-    norm_text(0, slot=2)
-    on_right[0].start()
-    to_left[2].wait_recv()
-    norm_text(2, slot=1)
-    on_left[0].start()
     for copy in kv_img:
         copy.wait_recv()
 

time: 56.2 us -> 56.2 us (level)
  no operation moved by 1% of the time
where the time goes in v8:
time: 56.2 us; the launch traced here: 56 us
  Pallas kernels  55.4 us (99%)
  between operations  0.65 us (1%)
    pallas_call x1, Pallas kernels, local(): pl.pallas_call(body, out_shape=out, in_specs=[hbm] * 10 + [vmem] * 2 + [s...  53.9 us
    pallas_call x1, Pallas kernels, local(): pl.pallas_call(unpack, out_shape=(single, single), in_specs=[vmem], out_s...  1.47 us

profile of v8, /device:TPU:0, one launch (start us, length us, event | category | flops | bytes accessed | tf_op | source)
XLA Modules:
  0.0 56.0 jit_solution(7025833803656867421)
XLA Ops:
  0.6 53.9 %guided_step.1.both = f32[2,64,128]{2,1,0:T(8,128)} custom-call(f32[64,256]{1,0:T(8,128)} %bitcast.15, bf16[128,3072]{1,0:T(8,128)(2,1)} %bitcast.12, bf16[64,3072]{1,0:T(8,128)(2,1)} %win_h.1, bf16[3072,1152]{1,0:T(8,128)(2,1)} %wq_h.1, bf16[3072,768]{1,0:T(8,128)(2,1)} %wt_h.1, bf16[1536,3072]{1,0:T(8,128)(2,1)} %wo_h.1, bf16[64,3072]{1,0:T(8,128)(2,1)} %bitcast.13, ...), custom_call_target="tpu_custom_call" | custom-call | tf_op jit(solution)/shard_map/guided_step/pallas_call | solution.py:471
  54.5 1.5 %unpack.1 = (f32[64,128]{1,0:T(8,128)}, f32[64,128]{1,0:T(8,128)}) custom-call(f32[2,64,128]{2,1,0:T(8,128)} %guided_step.1.both), custom_call_target="tpu_custom_call" | custom-call | tf_op jit(solution)/shard_map/unpack/pallas_call | solution.py:486
